TPU v7x, 32 devices: a whole 2x2x4 slice. The times are simulated.
32 devices in a mesh: row: 2 (over x), col: 4 (over y, core), freq: 4 (over z).
Axes of the slice: x: 2, y: 2, z: 4, core: 2. Of those that a mesh axis runs over, the one named last changes fastest.
Arguments:
- covariance: bfloat16 [16, 2, 4096, 4096], P('freq', None, 'row', 'col'), may hold values from -30 to 30, as said below
- replica_table: bfloat16 [16, 2, 4096, 512], P('freq', None, 'col'), may hold values from -18 to 18
- slab_index: int32 [384], replicated, may hold values from 0 to 511
Outputs:
- power: float32 [16, 384], P('freq', ('row', 'col'))
- surface: float32 [384], P(('row', 'col'))
Inputs may be any that keep to these rules, and one draw needn't show every extreme that they name: For each frequency, covariance is Hermitian: its real part is symmetric and its imaginary part antisymmetric, and the whole is positive definite.
All inputs are finite; a program needn't handle non-finite values.
Results may differ from a plain program's by a relative error of at most 0.0003.
Values may be sent and summed in bfloat16 or wider, within the bound.
No kernel may reach another device: no remote copies, remote signals or barrier semaphores. Data moves between devices by JAX's collectives and lax.ppermute only.
A program may use at most 192 MiB of HBM per device.

v0:
```python
import jax
import jax.numpy as jnp
from jax import lax
from jax.sharding import PartitionSpec as P

FREQ = 16


def broadcast(shard, axis, root):
    mine = lax.axis_index(axis) == root
    return lax.psum(jnp.where(mine, shard, jnp.zeros_like(shard)), axis)


def local(covariance, replica_table, slab_index):
    local_slab = jnp.take(replica_table, slab_index, axis=3)
    row_index = lax.axis_index("row")
    first_half = broadcast(local_slab, "col", 2 * row_index)
    second_half = broadcast(local_slab, "col", 2 * row_index + 1)
    row_slab = jnp.concatenate([first_half, second_half], axis=2)
    freqs = covariance.shape[0]
    rows_block = covariance.shape[2]
    cols_block = covariance.shape[3]
    slab = slab_index.shape[0]
    stacked = covariance.reshape(freqs, 2 * rows_block, cols_block)
    right_side = jnp.concatenate([local_slab[:, 0], local_slab[:, 1]], axis=2)
    image = jnp.einsum("fij,fjs->fis", stacked, right_side, preferred_element_type=jnp.float32)
    real_a = image[:, :rows_block, :slab]
    real_b = image[:, :rows_block, slab:]
    imag_a = image[:, rows_block:, :slab]
    imag_b = image[:, rows_block:, slab:]
    image_real = real_a - imag_b
    image_imag = real_b + imag_a
    quad = jnp.sum(
        row_slab[:, 0].astype(jnp.float32) * image_real
        + row_slab[:, 1].astype(jnp.float32) * image_imag,
        axis=1,
    )
    share = cols_block // lax.axis_size("row")
    own_piece = lax.dynamic_slice_in_dim(local_slab, row_index * share, share, 2).astype(
        jnp.float32
    )
    weight = jnp.sum(own_piece * own_piece, axis=(1, 2))
    quad_total, weight_total = (
        lax.psum_scatter(quad, ("row", "col"), scatter_dimension=1, tiled=True),
        lax.psum_scatter(weight, ("row", "col"), scatter_dimension=1, tiled=True),
    )
    power = quad_total / weight_total
    surface = lax.psum(jnp.sum(power, axis=0), "freq") / FREQ
    return (power, surface)


def solution(mesh):
    in_specs = (P("freq", None, "row", "col"), P("freq", None, "col", None), P())
    out_specs = (P("freq", ("row", "col")), P(("row", "col")))
    return jax.shard_map(local, mesh=mesh, in_specs=in_specs, out_specs=out_specs, check_vma=False)
```

profile of v0, /device:TPU:0, one launch (start us, length us, event | category | flops | bytes accessed | tf_op | source)
XLA Modules:
  0.0 369.8 jit_solution(8768695967303169388)
XLA Ops:
  8.0 0.0 all-reduce.3.cloned.1.call-start
  8.0 0.7 compare_and_fusion
  8.7 0.7 compare_select_fusion
  9.4 14.9 %copy.7 = bf16[4,2,1024,512]{2,0,1,3:T(4,128)(2,1)} copy(bf16[4,2,1024,512]{3,2,1,0:T(8,128)(2,1)} %param.4) | data formatting | bytes 16777216 | tf_op args[1]
  24.4 17.0 %gather_fusion = bf16[384,4,2,1024]{3,1,2,0:T(4,128)(2,1)} fusion(bf16[4,2,1024,512]{2,0,1,3:T(4,128)(2,1)} %copy.7, s32[1024]{0:T(1024)S(1)} %pad_clamp_fusion), kind=kCustom, calls=%fused_computation | custom fusion | bytes 12584448 | tf_op jit(solution)/shard_map/jit(_take)/gather | solution.py:15
  41.4 13.7 %broadcast_select_fusion = (bf16[4,2,1024,384]{2,3,0,1:T(8,128)(2,1)}, bf16[384,4,2,1024]{3,0,1,2:T(8,128)(2,1)S(1)}) fusion(pred[]{:T(512)S(6)} %eq.7, bf16[384,4,2,1024]{3,1,2,0:T(4,128)(2,1)} %gather_fusion, pred[384]{0:T(512)(128)(4,1)S(1)} %compare_and_fusion), kind=kLoop, calls=%fused_computation.15 | loop fusion | flops 6291456 | bytes 18874752 | tf_op jit(solution)/shard_map/jit(_where)/select_n | solution.py:11
  55.1 0.0 copy-start
  55.1 3.3 broadcast_select_fusion.1
  58.4 1.3 copy-done
  59.6 0.0 all-reduce.3.cloned.1.call-update
  59.7 0.0 reduce-scatter.9.cloned.1.call-start
  59.7 2.6 multiply_reduce_fusion
  62.3 0.8 copy.11
  63.1 0.0 reduce-scatter.9.cloned.1.call-update
  63.1 0.2 reduce-scatter.7.cloned.1.call-start
  63.4 5.8 %slice_bitcast_fusion.3 = (bf16[4,1024,384]{1,2,0:T(8,128)(2,1)S(1)}, bf16[4,1024,384]{1,2,0:T(8,128)(2,1)}) fusion(bf16[4,2,1024,384]{2,3,0,1:T(8,128)(2,1)} %bitcast.26), kind=kLoop, calls=%fused_computation.18 | loop fusion | bytes 12582912 | tf_op jit(solution)/shard_map/squeeze | solution.py:25
  69.1 38.6 %convolution_bitcast_fusion = f32[4,4096,768]{1,2,0:T(8,128)} fusion(bf16[4,4096,1024]{2,1,0:T(8,128)(2,1)} %bitcast.32, bf16[4,1024,384]{1,2,0:T(8,128)(2,1)} %get-tuple-element.9, bf16[4,1024,384]{1,2,0:T(8,128)(2,1)S(1)} %get-tuple-element.8), kind=kOutput, calls=%fused_computation.1 | convolution fusion | flops 25782386688 | bytes 90177536 | tf_op jit(solution)/shard_map/fij,fjs->fis/dot_general | solution.py:26
  107.7 176.3 %all-reduce.3.cloned.1.call-done = (bf16[4,2,1024,384]{2,3,0,1:T(8,128)(2,1)}, bf16[4,2,1024,384]{2,3,0,1:T(8,128)(2,1)}) async-done(((bf16[4,2,1024,384]{2,3,0,1:T(8,128)(2,1)}, bf16[4,2,1024,384]{2,3,0,1:T(8,128)(2,1)}), (bf16[4,2,1024,384]{2,3,0,1:T(8,128)(2,1)}, bf16[4,2,1024,384]{2,3,0,1:T(8,128)(2,1)})) %all-reduce.3.cloned.1.call-update) | async-done | bytes 12582928 | tf_op jit(solution)/shard_map/psum | solution.py:11
  284.0 0.0 copy-start.1
  284.0 6.3 %constant_dynamic-update-slice_fusion.1 = bf16[4,2,2048,384]{2,3,0,1:T(8,128)(2,1)} fusion(bf16[4,2,1024,384]{2,3,0,1:T(8,128)(2,1)} %get-tuple-element.2), kind=kLoop, calls=%fused_computation.22 | loop fusion | bytes 12582912
  290.3 0.0 copy-done.1
  290.3 3.3 constant_dynamic-update-slice_fusion
  293.6 20.4 %fusion.2 = f32[4,384]{1,0:T(4,128)S(1)} fusion(f32[4,4096,768]{1,2,0:T(8,128)} %convolution_bitcast_fusion, bf16[4,2,2048,384]{2,3,0,1:T(8,128)(2,1)} %constant_dynamic-update-slice_fusion), kind=kLoop, calls=%fused_computation.5 | loop fusion | flops 25164288 | bytes 62920704 | tf_op jit(solution)/shard_map/reduce_sum | solution.py:33
  314.0 0.8 copy.9
  314.9 0.0 reduce-scatter.7.cloned.1.call-update
  314.9 0.0 reduce-scatter.9.cloned.1.call-done
  314.9 0.8 copy.12
  315.7 33.1 %reduce-scatter.7.cloned.1.call-done = f32[48,4]{1,0:T(8,128)} async-done(((f32[384,4]{1,0:T(8,128)}), f32[48,4]{1,0:T(8,128)}) %reduce-scatter.7.cloned.1.call-update) | async-done | bytes 784
  348.8 0.8 copy.10
  349.6 0.6 fusion.8
  350.2 11.7 %psum.23 = f32[48]{0:T(128)S(1)} all-reduce(f32[48]{0:T(128)S(1)} %get-tuple-element.4), channel_id=1, replica_groups=mesh['row'=2,'col'=4,'freq'=4] {'freq'}, use_global_device_ids=true, to_apply=%region_7.8 | all-reduce | flops 48 | bytes 384 | tf_op jit(solution)/shard_map/psum | solution.py:48
  361.9 0.5 broadcast_multiply_fusion
  (1 shorter events, 0.0 us)
Async XLA Ops:
  8.0 276.0 %all-reduce.3.cloned.1.call-start = ((), (), s32[]{:S(2)}) async-start(), calls=%async_computation.4 | async-start | bytes 25165824 | tf_op jit(solution)/shard_map/psum | solution.py:11
  55.1 4.5 %copy-start = (bf16[384,4,2,1024]{3,0,1,2:T(8,128)(2,1)}, bf16[384,4,2,1024]{3,0,1,2:T(8,128)(2,1)S(1)}, u32[]{:S(2)}) copy-start(bf16[384,4,2,1024]{3,0,1,2:T(8,128)(2,1)S(1)} %get-tuple-element.7) | copy-start | bytes 18874372
  59.7 255.3 %reduce-scatter.9.cloned.1.call-start = ((), (), s32[]{:S(2)}) async-start(), calls=%async_computation.3 | async-start | bytes 221184
  63.1 285.7 %reduce-scatter.7.cloned.1.call-start = ((), (), s32[]{:S(2)}) async-start(), calls=%async_computation.2 | async-start | bytes 221184
  284.0 6.3 %copy-start.1 = (bf16[4,2,1024,384]{2,3,0,1:T(8,128)(2,1)S(1)}, bf16[4,2,1024,384]{2,3,0,1:T(8,128)(2,1)}, u32[]{:S(2)}) copy-start(bf16[4,2,1024,384]{2,3,0,1:T(8,128)(2,1)} %get-tuple-element.3) | copy-start | bytes 18874372
Sparse Core Ops, SparseCore 0:
  59.8 224.1 all-reduce.2
Sparse Core Ops, SparseCore 1:
  63.2 59.8 reduce-scatter.8
  315.0 33.8 reduce-scatter.6
where the time goes:
time: 371 us; the launch traced here: 370 us
  waiting for transfers between devices  209 us (56%)
  local copies, waits for them, and re-layouts  51.8 us (14%)
  other arithmetic  42.5 us (11%)
  matrix products  38.6 us (10%)
  between operations  15.5 us (4%)
  blocking collectives  11.7 us (3%)
    psum x1, waiting for transfers between devices, broadcast(): return lax.psum(jnp.where(mine, shard, jnp.zeros_like(shard)), axis)  176 us
    dot_general x1, matrix products, local(): jnp.einsum('fij,fjs->fis', stacked, right_side, preferred_element_type=jn...  38.6 us
    unnamed x5, waiting for transfers between devices  33.2 us
    unnamed x10, local copies, waits for them, and re-layouts  25.7 us
    reduce_sum x1, other arithmetic, local(): jnp.sum(row_slab[:, 0].astype(jnp.float32) * image_real + row_slab[:, 1]....  20.4 us
    select_n x2, other arithmetic, broadcast(): return lax.psum(jnp.where(mine, shard, jnp.zeros_like(shard)), axis)  17 us
    gather x1, local copies, waits for them, and re-layouts, local(): local_slab = jnp.take(replica_table, slab_index, axis=3)  17 us
    psum x1, blocking collectives, local(): surface = lax.psum(jnp.sum(power, axis=0), 'freq') / FREQ  11.7 us
  transfers between devices with their start and end apart: 3, of which 2 were waited for; matrix products, arithmetic and copies ran while one was open for 21% of the time, Pallas kernels for 0%

commit v1 on v0

v1 whole, which is shorter than its diff:
```python
import functools

import jax
import jax.numpy as jnp
from jax import lax
from jax.experimental import pallas as pl
from jax.experimental.pallas import tpu as pltpu
from jax.sharding import PartitionSpec as P


RELAYED = 2


class Place:
    def __init__(self, freqs):
        row, col = lax.axis_index("row"), lax.axis_index("col")
        chip, core = col // 2, col % 2
        half = freqs // 2
        self.diag = row == chip
        self.on = (row == chip).astype(jnp.int32)
        self.core = core
        self.first = jnp.where(row == chip, core, (row > chip).astype(jnp.int32)) * half
        self.other = half - self.first
        self.row, self.chip, self.half = row, chip, half

    def sends(self, d, rows):
        to = (self.row + d) % rows
        direct = (self.row > to).astype(jnp.int32) * self.half
        relay = (self.chip > self.row).astype(jnp.int32) * self.half + self.half // 2
        return jnp.where(self.diag, direct, relay)


def dot(x, y):
    return jnp.dot(x, y, preferred_element_type=jnp.float32)


def row_sum(x):
    return jnp.sum(x, axis=0, keepdims=True)


def onehot_of(index_ref, grid_points):
    slab = index_ref.shape[0]
    points = lax.broadcasted_iota(jnp.int32, (grid_points, slab), 0)
    hit = points == index_ref[...].reshape(1, slab)
    return jnp.where(hit, 1.0, 0.0).astype(jnp.bfloat16)


def pick_kernel(sizes, index_ref, main_ref, extra_ref, *out_refs):
    slab = index_ref.shape[0]
    onehot = onehot_of(index_ref, main_ref.shape[3])
    start = 0
    for size, out_ref in zip(sizes, out_refs, strict=True):
        twice = out_ref.shape[0] > size
        for part in range(2):
            columns = slice(part * slab, (part + 1) * slab)
            piece = dot(main_ref[0, part, start : start + size], onehot)
            out_ref[:size, columns] = piece.astype(jnp.bfloat16)
            if twice:
                piece = dot(extra_ref[0, part], onehot)
                out_ref[size:, columns] = piece.astype(jnp.bfloat16)
        start += size


def pick(index, table, d, rows, start, sizes, double_last):
    freqs, _, block, grid_points = table.shape
    slab = index.shape[0]
    height = sum(sizes)
    shapes = [(n, 2 * slab) for n in sizes]
    if double_last:
        shapes[-1] = (2 * sizes[-1], 2 * slab)
    extra = sizes[-1] if double_last else 16
    quarter = freqs // 4

    def main_at(i):
        return (Place(freqs).sends(d, rows), 0, start, 0)

    def extra_at(i):
        place = Place(freqs)
        return (jnp.where(place.diag, place.sends(d, rows) + quarter, 0), 0, block - extra, 0)

    def rows_of(height, at):
        element = pl.Element
        return pl.BlockSpec((element(1), element(2), element(height), element(grid_points)), at)

    return pl.pallas_call(
        functools.partial(pick_kernel, sizes),
        grid=(1,),
        in_specs=[pl.BlockSpec((slab,), lambda i: (0,)), rows_of(height, main_at), rows_of(extra, extra_at)],
        out_specs=[pl.BlockSpec(s, lambda i: (0, 0)) for s in shapes],
        out_shape=[jax.ShapeDtypeStruct(s, jnp.bfloat16) for s in shapes],
    )(index, table, table)


def gather_kernel(index_ref, table_ref, w_ref, norm_ref, onehot_ref):
    f = pl.program_id(0)
    slab = index_ref.shape[0]

    @pl.when(f == 0)
    def _():
        onehot_ref[...] = onehot_of(index_ref, table_ref.shape[3])

    total = jnp.zeros((1, slab), jnp.float32)
    for part in range(2):
        piece = dot(table_ref[0, part], onehot_ref[...])
        w_ref[0, :, part * slab : (part + 1) * slab] = piece.astype(jnp.bfloat16)
        total += row_sum(piece * piece)
    norm_ref[pl.ds(f, 1), :] = total


def gather(index, table):
    freqs, _, block, grid_points = table.shape
    slab = index.shape[0]
    return pl.pallas_call(
        gather_kernel,
        grid=(freqs,),
        in_specs=[
            pl.BlockSpec((slab,), lambda f: (0,)),
            pl.BlockSpec((1, 2, block, grid_points), lambda f: (f, 0, 0, 0)),
        ],
        out_specs=[
            pl.BlockSpec((1, block, 2 * slab), lambda f: (f, 0, 0)),
            pl.BlockSpec((freqs, slab), lambda f: (0, 0)),
        ],
        out_shape=[
            jax.ShapeDtypeStruct((freqs, block, 2 * slab), jnp.bfloat16),
            jax.ShapeDtypeStruct((freqs, slab), jnp.float32),
        ],
        scratch_shapes=[pltpu.VMEM((grid_points, slab), jnp.bfloat16)],
        name="gather",
    )(index, table)


def turned(w_ref, w2_ref, start=0):
    slab = w2_ref.shape[1] // 2
    w2_ref[start:, :slab] = -w_ref[0, start:, slab:]
    w2_ref[start:, slab:] = w_ref[0, start:, :slab]


def image_of(cov_ref, w_ref, w2_ref):
    turned(w_ref, w2_ref)
    return dot(cov_ref[0, 0], w_ref[0]) + dot(cov_ref[0, 1], w2_ref[...])


def send_kernel(cov_ref, w_ref, image_ref, w2_ref):
    image_ref[0] = image_of(cov_ref, w_ref, w2_ref)


def send_images(covariance, w):
    freqs, block, wide = w.shape
    half = freqs // 2

    def cov_at(i):
        place = Place(freqs)
        return (place.first + i, 0, 1 - place.core, 0)

    return pl.pallas_call(
        send_kernel,
        grid=(half,),
        in_specs=[
            pl.BlockSpec((1, 2, block, block), cov_at),
            pl.BlockSpec((1, block, wide), lambda i: (Place(freqs).first + i, 0, 0)),
        ],
        out_specs=pl.BlockSpec((1, block, wide), lambda i: (i, 0, 0)),
        scratch_shapes=[pltpu.VMEM((block, wide), jnp.bfloat16)],
        out_shape=jax.ShapeDtypeStruct((half, block, wide), jnp.float32),
        name="send_images",
    )(covariance, w)


def own_form(cov_ref, w_ref, w2_ref):
    block, wide = w2_ref.shape
    slab = wide // 2
    tile = block // 2
    turned(w_ref, w2_ref, tile)
    total = jnp.zeros((1, wide), jnp.float32)
    for t in range(2):
        rows = slice(t * tile, (t + 1) * tile)
        left = w_ref[0, rows].astype(jnp.float32)
        image = dot(cov_ref[0, 0, rows, rows], w_ref[0, rows])
        cross = dot(cov_ref[0, 1, rows, rows], w_ref[0, rows, :slab])
        if t == 0:
            rest = slice(tile, block)
            upper = dot(cov_ref[0, 0, rows, rest], w_ref[0, rest])
            upper += dot(cov_ref[0, 1, rows, rest], w2_ref[rest])
            image += 2.0 * upper
        total += row_sum(left * image)
        twice = 2.0 * row_sum(left[:, slab:] * cross)
        total += jnp.concatenate([twice, jnp.zeros_like(twice)], axis=1)
    return total


def keep_kernel(cov_ref, w_ref, image_ref, quad_ref, w2_ref):
    i = pl.program_id(0)
    freqs = quad_ref.shape[0]
    place = Place(freqs)

    @pl.when(i == 0)
    def _():
        quad_ref[...] = jnp.zeros_like(quad_ref)

    @pl.when(place.diag)
    def _():
        quad_ref[pl.ds(i, 1), :] = own_form(cov_ref, w_ref, w2_ref)

    @pl.when(jnp.logical_not(place.diag) & (i < freqs // 2))
    def _():
        image_ref[0] = image_of(cov_ref, w_ref, w2_ref)


def keep_images(covariance, w):
    freqs, block, wide = w.shape
    half = freqs // 2

    def freq_at(i):
        place = Place(freqs)
        return jnp.where(place.diag, i, place.first + jnp.minimum(i, half - 1))

    return pl.pallas_call(
        keep_kernel,
        grid=(freqs,),
        in_specs=[
            pl.BlockSpec((1, 2, block, block), lambda i: (freq_at(i), 0, Place(freqs).core, 0)),
            pl.BlockSpec((1, block, wide), lambda i: (freq_at(i), 0, 0)),
        ],
        out_specs=[
            pl.BlockSpec(
                (1, block, wide), lambda i: (jnp.minimum(i, half - 1) * (1 - Place(freqs).on), 0, 0)
            ),
            pl.BlockSpec((freqs, wide), lambda i: (0, 0)),
        ],
        scratch_shapes=[pltpu.VMEM((block, wide), jnp.bfloat16)],
        out_shape=[
            jax.ShapeDtypeStruct((half, block, wide), jnp.float32),
            jax.ShapeDtypeStruct((freqs, wide), jnp.float32),
        ],
        name="keep_images",
    )(covariance, w)


def fetch_all(pieces, keep_ref, received_ref, buffers, sems):
    copies = []
    for k, (_, _, rows, item, row) in enumerate(pieces):
        for s, side in enumerate((keep_ref, received_ref)):
            copy = pltpu.make_async_copy(side.at[item, pl.ds(row, rows)], buffers[2 * k + s], sems.at[2 * k + s])
            copy.start()
            copies.append(copy)
    return copies


def add_far(pieces, lefts, copies, buffers, quad_ref, first):
    for k, (source, at, rows, item, _) in enumerate(pieces):
        for s in range(2):
            copies[2 * k + s].wait()
        left = lefts[source][at : at + rows].astype(jnp.float32)
        value = 2.0 * row_sum(left * (buffers[2 * k][...] + buffers[2 * k + 1][...]))
        quad_ref[pl.ds(first + item, 1), :] += value


def early_kernel(pieces, n_left, quad_in_ref, w_ref, keep_ref, received_ref, *refs):
    lefts, (out_ref, w_buffer, image_buffer, own_sems, sems), buffers = (
        refs[:n_left],
        refs[n_left : n_left + 5],
        refs[n_left + 5 :],
    )
    freqs, half = w_ref.shape[0], received_ref.shape[0]
    place = Place(freqs)
    out_ref[...] = quad_in_ref[...]

    @pl.when(place.diag)
    def _():
        copies = []
        for i in range(half):
            copies.append(pltpu.make_async_copy(w_ref.at[place.other + i], w_buffer.at[i], own_sems.at[2 * i]))
            copies.append(pltpu.make_async_copy(received_ref.at[i], image_buffer.at[i], own_sems.at[2 * i + 1]))
        for copy in copies:
            copy.start()
        for i in range(half):
            copies[2 * i].wait()
            copies[2 * i + 1].wait()
            value = 2.0 * row_sum(w_buffer[i].astype(jnp.float32) * image_buffer[i])
            out_ref[pl.ds(place.other + i, 1), :] += value

    @pl.when(jnp.logical_not(place.diag))
    def _():
        copies = fetch_all(pieces, keep_ref, received_ref, buffers, sems)
        add_far(pieces, lefts, copies, buffers, out_ref, place.first)


HBM = pl.BlockSpec(memory_space=pltpu.HBM)
VMEM = pl.BlockSpec(memory_space=pltpu.VMEM)


def piece_buffers(pieces, wide):
    return [pltpu.VMEM((p[2], wide), jnp.float32) for p in pieces for _ in range(2)]


def early_dots(quad, w, keep, received, lefts, pieces):
    _, block, wide = w.shape
    half = received.shape[0]
    return pl.pallas_call(
        functools.partial(early_kernel, pieces, len(lefts)),
        in_specs=[VMEM, HBM, HBM, HBM] + [VMEM] * len(lefts),
        out_specs=VMEM,
        scratch_shapes=[
            pltpu.VMEM((half, block, wide), jnp.bfloat16),
            pltpu.VMEM((half, block, wide), jnp.float32),
            pltpu.SemaphoreType.DMA((2 * half,)),
            pltpu.SemaphoreType.DMA((2 * len(pieces),)),
            *piece_buffers(pieces, wide),
        ],
        out_shape=jax.ShapeDtypeStruct(quad.shape, jnp.float32),
        name="early_dots",
    )(quad, w, keep, received, *lefts)


def late_kernel(pieces, n_left, planes, quad_in_ref, norm_ref, keep_ref, received_ref, *refs):
    lefts, (out_ref, quad_ref, sems), buffers = refs[:n_left], refs[n_left : n_left + 3], refs[n_left + 3 :]
    freqs, slab = norm_ref.shape
    place = Place(freqs)
    quad_ref[...] = quad_in_ref[...]

    @pl.when(jnp.logical_not(place.diag))
    def _():
        copies = fetch_all(pieces, keep_ref, received_ref, buffers, sems)
        add_far(pieces, lefts, copies, buffers, quad_ref, place.first)

    both = jnp.concatenate([quad_ref[:, :slab] + quad_ref[:, slab:], norm_ref[...]], axis=0)
    own = out_ref.shape[2]
    for owner in range(out_ref.shape[0] // planes):
        parcel = both[:, owner * own : (owner + 1) * own]
        for z in range(planes):
            out_ref[owner * planes + z] = parcel


def late_dots(quad, norm, keep, received, lefts, pieces, owners, planes):
    freqs, slab = norm.shape
    wide = quad.shape[1]
    return pl.pallas_call(
        functools.partial(late_kernel, pieces, len(lefts), planes),
        in_specs=[VMEM, VMEM, HBM, HBM] + [VMEM] * len(lefts),
        out_specs=VMEM,
        scratch_shapes=[
            pltpu.VMEM((freqs, wide), jnp.float32),
            pltpu.SemaphoreType.DMA((2 * len(pieces),)),
            *piece_buffers(pieces, wide),
        ],
        out_shape=jax.ShapeDtypeStruct((owners * planes, 2 * freqs, slab // owners), jnp.float32),
        name="late_dots",
    )(quad, norm, keep, received, *lefts)


def finish_kernel(planes, copies, arrived_ref, power_ref, surface_ref):
    freqs = power_ref.shape[0]
    mine = lax.axis_index("freq")
    surface = jnp.zeros_like(surface_ref)
    for z in range(planes):
        total = arrived_ref[z]
        for source in range(1, arrived_ref.shape[0] // planes):
            total += arrived_ref[source * planes + z]
        power = total[:freqs] / (total[freqs:] * (1.0 / copies))
        surface += row_sum(power)

        @pl.when(mine == z)
        def _():
            power_ref[...] = power

    surface_ref[...] = surface / (freqs * planes)


def finish(arrived, planes, copies):
    _, twice, own = arrived.shape
    return pl.pallas_call(
        functools.partial(finish_kernel, planes, copies),
        in_specs=[VMEM],
        out_specs=[VMEM, VMEM],
        out_shape=[
            jax.ShapeDtypeStruct((twice // 2, own), jnp.float32),
            jax.ShapeDtypeStruct((1, own), jnp.float32),
        ],
        name="finish",
    )(arrived)


def local(mesh, covariance, replica_table, slab_index):
    rows, cols, planes = (mesh.shape[a] for a in ("row", "col", "freq"))
    freqs, _, row_block, block = covariance.shape
    chips = cols // 2
    if row_block != 2 * block or chips != rows or freqs != 4:
        raise ValueError("unsupported mesh")
    axes = ("row", "col")

    def device(r, q, j):
        return r * cols + 2 * q + j

    def move(x, pairs):
        return lax.ppermute(x, axes, pairs)

    def total(xs):
        return functools.reduce(jnp.add, xs)

    everyone = [(r, q, j) for r in range(rows) for q in range(chips) for j in range(2)]
    core_swap = [(device(r, q, j), device(r, q, 1 - j)) for r, q, j in everyone]

    n = RELAYED
    chunk = block * 2 // 5 // 16 * 16
    tail = block - n * chunk
    shifts = range(1, rows)
    pairs = {}
    for d in shifts:
        out, back, relay = [], [], []
        for r in range(rows):
            for j in range(2):
                other = (r + d) % rows
                out.append((device(r, r, j), device(r, other, j)))
                back.append((device(r, other, j), device(r, r, j)))
                relay.append((device(r, r, j), device(other, r, j)))
        pairs[d] = out, out + back, relay

    chunks, hops = {}, {}
    for d in shifts:
        chunks[d] = pick(slab_index, replica_table, d, rows, 0, [chunk], False)
        hops[d] = [move(chunks[d][0], pairs[d][1])]
    for d in shifts:
        sizes = [chunk] * (n - 1) + [tail]
        chunks[d] += pick(slab_index, replica_table, d, rows, chunk, sizes, True)
        for k in range(1, n + 1):
            hops[d].append(move(chunks[d][k], pairs[d][1 if k < n else 0]))

    w, norm = gather(slab_index, replica_table)
    sent = send_images(covariance, w)
    received = move(sent, core_swap)
    relayed = [total([move(hops[d][k], pairs[d][2]) for d in shifts]) for k in range(n)]
    direct = [total([hops[d][k] for d in shifts]) for k in range(n + 1)]
    keep, quad = keep_images(covariance, w)
    early = [(k, 0, chunk, 0, k * chunk) for k in range(n)]
    early += [(n + k, 0, chunk, 1, k * chunk) for k in range(n - 1)]
    late = [(0, 0, tail, 0, n * chunk), (0, tail, tail, 1, n * chunk), (1, 0, chunk, 1, (n - 1) * chunk)]
    quad = early_dots(quad, w, keep, received, direct[:n] + relayed[: n - 1], early)
    parcels = late_dots(
        quad, norm, keep, received, [direct[n], relayed[-1]], late, rows * cols, planes
    )
    arrived = lax.all_to_all(parcels, ("row", "col", "freq"), 0, 0)
    power, surface = finish(arrived, planes, rows)
    return power, surface[0]


def solution(mesh):
    in_specs = (P("freq", None, "row", "col"), P("freq", None, "col", None), P())
    out_specs = (P("freq", ("row", "col")), P(("row", "col")))

    def body(covariance, replica_table, slab_index):
        return local(mesh, covariance, replica_table, slab_index)

    return jax.shard_map(body, mesh=mesh, in_specs=in_specs, out_specs=out_specs, check_vma=False)
```

time: 371 us -> 101 us (0.27)
  waiting for transfers between devices: 209 us -> 16.6 us
  Pallas kernels: 0 us -> 51.2 us
  local copies, waits for them, and re-layouts: 51.8 us -> 4.19 us
  other arithmetic: 42.5 us -> 0.76 us
  matrix products: 38.6 us -> 0 us
  between operations: 15.5 us -> 0.75 us
  starting transfers between devices: 0.31 us -> 15 us
    psum x1 -> x0, waiting for transfers between devices: 176 us -> none  [broadcast(): return lax.psum(jnp.where(mine, shard, jnp.zeros_like(shard)), axis)]
    pallas_call x0 -> x8, Pallas kernels: none -> 51.2 us  [the longest x1 14.5 us: keep_images(): pl.pallas_call(keep_kernel, grid=(freqs,), in_specs=[pl.BlockSpec((1, 2,...]
    dot_general x1 -> x0, matrix products: 38.6 us -> none  [local(): jnp.einsum('fij,fjs->fis', stacked, right_side, preferred_element_type=jn...]
    unnamed x5 -> x0, waiting for transfers between devices: 33.2 us -> none
    reduce_sum x3 -> x0, other arithmetic: 23.6 us -> none  [the longest x1 20.4 us: local(): jnp.sum(row_slab[:, 0].astype(jnp.float32) * image_real + row_slab[:, 1]....]
    unnamed x10 -> x12, local copies, waits for them, and re-layouts: 25.7 us -> 3.68 us
    select_n x3 -> x0, other arithmetic: 17.7 us -> none  [the longest x2 17 us: broadcast(): return lax.psum(jnp.where(mine, shard, jnp.zeros_like(shard)), axis)]
    gather x1 -> x0, local copies, waits for them, and re-layouts: 17 us -> none  [local(): local_slab = jnp.take(replica_table, slab_index, axis=3)]
  transfers between devices with their start and end apart: 3 -> 6, of which waited for: 2 -> 2; matrix products, arithmetic and copies ran while one was open for 21% -> 0% of each run, Pallas kernels for 0% -> 27%
where the time goes in v1:
time: 101 us
  Pallas kernels  51.2 us (51%)
  waiting for transfers between devices  16.6 us (16%)
  starting transfers between devices  15 us (15%)
  blocking collectives  12.1 us (12%)
  local copies, waits for them, and re-layouts  4.19 us (4%)
    ppermute x6, waiting for transfers between devices, move(): return lax.ppermute(x, axes, pairs)  16.6 us
    ppermute x6, starting transfers between devices, move(): return lax.ppermute(x, axes, pairs)  15 us
    pallas_call x1, Pallas kernels, keep_images(): pl.pallas_call(keep_kernel, grid=(freqs,), in_specs=[pl.BlockSpec((1, 2,...  14.5 us
    all_to_all x1, blocking collectives, local(): arrived = lax.all_to_all(parcels, ('row', 'col', 'freq'), 0, 0)  12.1 us
    pallas_call x1, Pallas kernels, send_images(): pl.pallas_call(send_kernel, grid=(half,), in_specs=[pl.BlockSpec((1, 2, b...  11.4 us
    pallas_call x1, Pallas kernels, gather(): pl.pallas_call(gather_kernel, grid=(freqs,), in_specs=[pl.BlockSpec((slab...  8.99 us
    pallas_call x1, Pallas kernels, early_dots(): pl.pallas_call(functools.partial(early_kernel, pieces, len(lefts)), in_sp...  6.53 us
    pallas_call x2, Pallas kernels, pick(): pl.pallas_call(functools.partial(pick_kernel, sizes), grid=(1,), in_specs...  6.02 us
  transfers between devices with their start and end apart: 6, of which 2 were waited for; matrix products, arithmetic and copies ran while one was open for 0% of the time, Pallas kernels for 27%

profile of v1, /device:TPU:0, one launch (start us, length us, event | category | flops | bytes accessed | tf_op | source)
XLA Modules:
  0.0 100.5 jit_solution(8634306691258629206)
XLA Ops:
  0.6 9.0 %gather.1 = (bf16[4,1024,768]{2,1,0:T(8,128)(2,1)}, f32[4,384]{1,0:T(4,128)}) custom-call(s32[384]{0:T(512)} %index_ref.5, bf16[4,2,1024,512]{3,2,1,0:T(8,128)(2,1)} %extra_ref.3), custom_call_target="tpu_custom_call" | custom-call | tf_op jit(solution)/shard_map/gather/pallas_call | solution.py:113
  9.6 11.4 %send_images.1 = f32[2,1024,768]{2,1,0:T(8,128)} custom-call(bf16[4,2,2048,1024]{3,2,1,0:T(8,128)(2,1)} %cov_ref.3, bf16[4,1024,768]{2,1,0:T(8,128)(2,1)} %get-tuple-element.10.w_ref), custom_call_target="tpu_custom_call" | custom-call | tf_op jit(solution)/shard_map/send_images/pallas_call | solution.py:156
  21.0 0.5 collective-permute-start
  21.5 2.6 %shard_map.50 = bf16[400,768]{1,0:T(8,128)(2,1)} custom-call(s32[384]{0:T(512)} %index_ref.5, bf16[4,2,1024,512]{3,2,1,0:T(8,128)(2,1)} %extra_ref.3, bf16[4,2,1024,512]{3,2,1,0:T(8,128)(2,1)} %extra_ref.3), custom_call_target="tpu_custom_call" | custom-call | tf_op jit(solution)/shard_map/pallas_call | solution.py:85
  24.1 2.5 %collective-permute-start.1 = (bf16[400,768]{1,0:T(8,128)(2,1)}, bf16[400,768]{1,0:T(8,128)(2,1)S(1)}, u32[]{:S(2)}, u32[]{:S(2)}) collective-permute-start(bf16[400,768]{1,0:T(8,128)(2,1)} %shard_map.50), channel_id=1, source_target_pairs={{0,8},{4,12},{24,16},{28,20},{8,0},{12,4},{16,24},{20,28},{1,9},{5... | collective-permute-start | bytes 1843208 | tf_op jit(solution)/shard_map/ppermute | solution.py:396
  26.6 3.4 %shard_map.51 = (bf16[400,768]{1,0:T(8,128)(2,1)}, bf16[448,768]{1,0:T(8,128)(2,1)}) custom-call(s32[384]{0:T(512)} %index_ref.5, bf16[4,2,1024,512]{3,2,1,0:T(8,128)(2,1)} %extra_ref.3, bf16[4,2,1024,512]{3,2,1,0:T(8,128)(2,1)} %extra_ref.3), custom_call_target="tpu_custom_call" | custom-call | tf_op jit(solution)/shard_map/pallas_call | solution.py:85
  30.0 0.0 collective-permute-start.2
  30.0 4.0 %collective-permute-start.4 = (bf16[448,768]{1,0:T(8,128)(2,1)}, bf16[448,768]{1,0:T(8,128)(2,1)S(1)}, u32[]{:S(2)}, u32[]{:S(2)}) collective-permute-start(bf16[448,768]{1,0:T(8,128)(2,1)} %get-tuple-element.15), channel_id=1, source_target_pairs={{0,8},{4,12},{24,16},{28,20},{1,9},{5,13},{25,17},{29,21},{2,10},{... | collective-permute-start | bytes 2064392 | tf_op jit(solution)/shard_map/ppermute | solution.py:396
  34.0 7.5 %collective-permute-done.1.refs_0_ = bf16[400,768]{1,0:T(8,128)(2,1)S(1)} collective-permute-done((bf16[400,768]{1,0:T(8,128)(2,1)}, bf16[400,768]{1,0:T(8,128)(2,1)S(1)}, u32[]{:S(2)}, u32[]{:S(2)}) %collective-permute-start.1) | collective-permute-done | bytes 614432 | tf_op jit(solution)/shard_map/ppermute | solution.py:396
  41.5 3.9 %collective-permute-start.3 = (bf16[400,768]{1,0:T(8,128)(2,1)S(1)}, bf16[400,768]{1,0:T(8,128)(2,1)S(1)}, u32[]{:S(2)}, u32[]{:S(2)}) collective-permute-start(bf16[400,768]{1,0:T(8,128)(2,1)S(1)} %collective-permute-done.1.refs_0_), channel_id=1, source_target_pairs={{0,16},{4,20},{24,8},{28,12},{1,17},{5,21},{25,9},{29,13},{2,18},{... | collective-permute-start | bytes 1843208 | tf_op jit(solution)/shard_map/ppermute | solution.py:396
  45.5 9.0 %collective-permute-done.2.refs_1_ = bf16[400,768]{1,0:T(8,128)(2,1)S(1)} collective-permute-done((bf16[400,768]{1,0:T(8,128)(2,1)}, bf16[400,768]{1,0:T(8,128)(2,1)S(1)}, u32[]{:S(2)}, u32[]{:S(2)}) %collective-permute-start.2) | collective-permute-done | bytes 614432 | tf_op jit(solution)/shard_map/ppermute | solution.py:396
  54.5 4.1 %collective-permute-start.5 = (bf16[400,768]{1,0:T(8,128)(2,1)S(1)}, bf16[400,768]{1,0:T(8,128)(2,1)S(1)}, u32[]{:S(2)}, u32[]{:S(2)}) collective-permute-start(bf16[400,768]{1,0:T(8,128)(2,1)S(1)} %collective-permute-done.2.refs_1_), channel_id=1, source_target_pairs={{0,16},{4,20},{24,8},{28,12},{1,17},{5,21},{25,9},{29,13},{2,18},{... | collective-permute-start | bytes 1843208 | tf_op jit(solution)/shard_map/ppermute | solution.py:396
  58.6 14.5 %keep_images.1 = (f32[2,1024,768]{2,1,0:T(8,128)}, f32[4,768]{1,0:T(4,128)}) custom-call(bf16[4,2,2048,1024]{3,2,1,0:T(8,128)(2,1)} %cov_ref.3, bf16[4,1024,768]{2,1,0:T(8,128)(2,1)} %get-tuple-element.10.w_ref), custom_call_target="tpu_custom_call" | custom-call | tf_op jit(solution)/shard_map/keep_images/pallas_call | solution.py:218
  73.2 0.0 copy-done.1
  73.2 0.0 copy-done.2
  73.2 0.0 collective-permute-done.3.refs_2_
  73.2 0.0 copy-start.3
  73.2 0.0 collective-permute-done.received_ref
  73.2 0.8 copy-done.3
  74.0 6.5 %early_dots.1.quad_in_ref = f32[4,768]{1,0:T(4,128)} custom-call(f32[4,768]{1,0:T(4,128)} %get-tuple-element.11.quad_in_ref, bf16[4,1024,768]{2,1,0:T(8,128)(2,1)} %get-tuple-element.10.w_ref, f32[2,1024,768]{2,1,0:T(8,128)} %get-tuple-element.12.keep_ref, f32[2,1024,768]{2,1,0:T(8,128)} %collective-permute-done.received_ref, bf16[400,768]{1,0:T(8,128)(2,1)} %copy-done.1, ...), custom_call_target="tpu_custom_call" | custom-call | tf_op jit(solution)/shard_map/early_dots/pallas_call | solution.py:300
  80.6 0.0 collective-permute-done.4.refs_0_
  80.6 0.0 copy-start
  80.6 0.0 collective-permute-done.5.refs_1_
  80.6 0.8 copy-done
  81.5 0.2 copy-done.4
  81.7 2.1 %late_dots.1 = f32[32,8,48]{2,1,0:T(8,128)} custom-call(f32[4,768]{1,0:T(4,128)} %early_dots.1.quad_in_ref, f32[4,384]{1,0:T(4,128)} %get-tuple-element.14.norm_ref, f32[2,1024,768]{2,1,0:T(8,128)} %get-tuple-element.12.keep_ref, f32[2,1024,768]{2,1,0:T(8,128)} %collective-permute-done.received_ref, bf16[448,768]{1,0:T(8,128)(2,1)} %copy-done, ...), custom_call_target="tpu_custom_call" | custom-call | tf_op jit(solution)/shard_map/late_dots/pallas_call | solution.py:338
  83.8 1.1 %reshape.4 = f32[32,1,384]{2,1,0:T(1,128)S(1)} reshape(f32[32,8,48]{2,1,0:T(8,128)} %late_dots.1) | data formatting | bytes 98304
  84.8 12.1 %all_to_all.5 = f32[32,1,384]{2,1,0:T(1,128)S(1)} all-to-all(f32[32,1,384]{2,1,0:T(1,128)S(1)} %reshape.4), channel_id=1, replica_groups=mesh['row'=2,'col'=4,'freq'=4] {'row','col','freq'}, dimensions={0} | all-to-all | bytes 98304 | tf_op jit(solution)/shard_map/all_to_all | solution.py:442
  96.9 0.5 broadcast
  97.4 0.8 reduce
  98.2 0.8 reshape.5.arrived_ref
  99.0 1.6 %finish.1 = (f32[4,48]{1,0:T(4,128)}, f32[1,48]{1,0:T(1,128)}) custom-call(f32[32,8,48]{2,1,0:T(8,128)} %reshape.5.arrived_ref), custom_call_target="tpu_custom_call" | custom-call | tf_op jit(solution)/shard_map/finish/pallas_call | solution.py:372
  (3 shorter events, 0.0 us)
Async XLA Ops:
  21.0 52.2 %collective-permute-start = (f32[2,1024,768]{2,1,0:T(8,128)}, f32[2,1024,768]{2,1,0:T(8,128)}, u32[]{:S(2)}, u32[]{:S(2)}) collective-permute-start(f32[2,1024,768]{2,1,0:T(8,128)} %send_images.1), channel_id=1, source_target_pairs={{0,4},{4,0},{8,12},{12,8},{16,20},{20,16},{24,28},{28,24},{1,5},{5... | collective-permute-start | bytes 18874376 | tf_op jit(solution)/shard_map/ppermute | solution.py:396
  24.1 17.4 %collective-permute-start.1 = (bf16[400,768]{1,0:T(8,128)(2,1)}, bf16[400,768]{1,0:T(8,128)(2,1)S(1)}, u32[]{:S(2)}, u32[]{:S(2)}) collective-permute-start(bf16[400,768]{1,0:T(8,128)(2,1)} %shard_map.50), channel_id=1, source_target_pairs={{0,8},{4,12},{24,16},{28,20},{8,0},{12,4},{16,24},{20,28},{1,9},{5... | collective-permute-start | bytes 1843208 | tf_op jit(solution)/shard_map/ppermute | solution.py:396
  30.0 24.5 %collective-permute-start.2 = (bf16[400,768]{1,0:T(8,128)(2,1)}, bf16[400,768]{1,0:T(8,128)(2,1)S(1)}, u32[]{:S(2)}, u32[]{:S(2)}) collective-permute-start(bf16[400,768]{1,0:T(8,128)(2,1)} %get-tuple-element.13), channel_id=1, source_target_pairs={{0,8},{4,12},{24,16},{28,20},{8,0},{12,4},{16,24},{20,28},{1,9},{5... | collective-permute-start | bytes 1843208 | tf_op jit(solution)/shard_map/ppermute | solution.py:396
  30.0 50.6 %collective-permute-start.4 = (bf16[448,768]{1,0:T(8,128)(2,1)}, bf16[448,768]{1,0:T(8,128)(2,1)S(1)}, u32[]{:S(2)}, u32[]{:S(2)}) collective-permute-start(bf16[448,768]{1,0:T(8,128)(2,1)} %get-tuple-element.15), channel_id=1, source_target_pairs={{0,8},{4,12},{24,16},{28,20},{1,9},{5,13},{25,17},{29,21},{2,10},{... | collective-permute-start | bytes 2064392 | tf_op jit(solution)/shard_map/ppermute | solution.py:396
  41.5 31.6 %copy-start.1 = (bf16[400,768]{1,0:T(8,128)(2,1)}, bf16[400,768]{1,0:T(8,128)(2,1)S(1)}, u32[]{:S(2)}) copy-start(bf16[400,768]{1,0:T(8,128)(2,1)S(1)} %collective-permute-done.1.refs_0_) | copy-start | bytes 1843204
  41.5 31.7 %collective-permute-start.3 = (bf16[400,768]{1,0:T(8,128)(2,1)S(1)}, bf16[400,768]{1,0:T(8,128)(2,1)S(1)}, u32[]{:S(2)}, u32[]{:S(2)}) collective-permute-start(bf16[400,768]{1,0:T(8,128)(2,1)S(1)} %collective-permute-done.1.refs_0_), channel_id=1, source_target_pairs={{0,16},{4,20},{24,8},{28,12},{1,17},{5,21},{25,9},{29,13},{2,18},{... | collective-permute-start | bytes 1843208 | tf_op jit(solution)/shard_map/ppermute | solution.py:396
  54.5 18.7 %copy-start.2 = (bf16[400,768]{1,0:T(8,128)(2,1)}, bf16[400,768]{1,0:T(8,128)(2,1)S(1)}, u32[]{:S(2)}) copy-start(bf16[400,768]{1,0:T(8,128)(2,1)S(1)} %collective-permute-done.2.refs_1_) | copy-start | bytes 1843204
  54.5 26.1 %collective-permute-start.5 = (bf16[400,768]{1,0:T(8,128)(2,1)S(1)}, bf16[400,768]{1,0:T(8,128)(2,1)S(1)}, u32[]{:S(2)}, u32[]{:S(2)}) collective-permute-start(bf16[400,768]{1,0:T(8,128)(2,1)S(1)} %collective-permute-done.2.refs_1_), channel_id=1, source_target_pairs={{0,16},{4,20},{24,8},{28,12},{1,17},{5,21},{25,9},{29,13},{2,18},{... | collective-permute-start | bytes 1843208 | tf_op jit(solution)/shard_map/ppermute | solution.py:396
  73.2 0.9 copy-start.3
  80.6 0.9 copy-start
  80.6 1.0 %copy-start.4 = (bf16[400,768]{1,0:T(8,128)(2,1)}, bf16[400,768]{1,0:T(8,128)(2,1)S(1)}, u32[]{:S(2)}) copy-start(bf16[400,768]{1,0:T(8,128)(2,1)S(1)} %collective-permute-done.5.refs_1_) | copy-start | bytes 1843204

commit v2 on v1

v2 whole, which is shorter than its diff:
```python
import functools

import jax
import jax.numpy as jnp
from jax import lax
from jax.experimental import pallas as pl
from jax.experimental.pallas import tpu as pltpu
from jax.sharding import PartitionSpec as P


CHUNKS = (4, 5, 4)
RELAYED = len(CHUNKS)


PARAMS = pltpu.CompilerParams(vmem_limit_bytes=30 << 20)


HBM = pl.BlockSpec(memory_space=pltpu.HBM)
VMEM = pl.BlockSpec(memory_space=pltpu.VMEM)


def apart(x):
    return pltpu.with_memory_space_constraint(x, pltpu.HBM)


def resident(x):
    return pltpu.with_memory_space_constraint(x, pltpu.VMEM)


class Place:
    def __init__(self, freqs):
        row, col = lax.axis_index("row"), lax.axis_index("col")
        chip, core = col // 2, col % 2
        half = freqs // 2
        self.diag = row == chip
        self.on = (row == chip).astype(jnp.int32)
        self.core = core
        self.first = jnp.where(row == chip, core, (row > chip).astype(jnp.int32)) * half
        self.other = half - self.first
        self.row, self.chip, self.half = row, chip, half

    def sends(self, d, rows):
        to = (self.row + d) % rows
        direct = (self.row > to).astype(jnp.int32) * self.half
        relay = (self.chip > self.row).astype(jnp.int32) * self.half + self.half // 2
        return jnp.where(self.diag, direct, relay)


def dot(x, y):
    return jnp.dot(x, y, preferred_element_type=jnp.float32)


def row_sum(x):
    return jnp.sum(x, axis=0, keepdims=True)


def folded(rows, wide, product):
    def step(k, total):
        part = product(pl.multiple_of(k * 16, 16), 16)
        return total + (part[:8] + part[8:])

    return row_sum(lax.fori_loop(0, rows // 16, step, jnp.zeros((8, wide), jnp.float32), unroll=4))


def onehot_of(index_ref, grid_points):
    slab = index_ref.shape[0]
    points = lax.broadcasted_iota(jnp.int32, (grid_points, slab), 0)
    hit = points == index_ref[...].reshape(1, slab)
    return jnp.where(hit, 1.0, 0.0).astype(jnp.bfloat16)


def pick_kernel(sizes, index_ref, main_ref, *refs):
    slab = index_ref.shape[0]
    extra_ref, out_refs = (refs[0], refs[1:]) if len(refs) > len(sizes) else (None, refs)
    onehot = onehot_of(index_ref, main_ref.shape[3])
    start = 0
    for size, out_ref in zip(sizes, out_refs, strict=True):
        for part in range(2):
            columns = slice(part * slab, (part + 1) * slab)
            piece = dot(main_ref[0, part, start : start + size], onehot)
            out_ref[:size, columns] = piece.astype(jnp.bfloat16)
            if out_ref.shape[0] > size:
                piece = dot(extra_ref[0, part], onehot)
                out_ref[size:, columns] = piece.astype(jnp.bfloat16)
        start += size


def pick(index, table, d, rows, start, sizes, double_last):
    freqs, _, _, grid_points = table.shape
    slab = index.shape[0]
    shapes = [(n, 2 * slab) for n in sizes]
    height = sum(sizes)
    extra = sizes[-1]
    quarter = freqs // 4

    def main_at(i):
        return (Place(freqs).sends(d, rows), 0, start, 0)

    def extra_at(i):
        place = Place(freqs)
        return (jnp.where(place.diag, place.sends(d, rows) + quarter, 0), 0, start + height - extra, 0)

    def rows_of(height, at):
        element = pl.Element
        return pl.BlockSpec((element(1), element(2), element(height), element(grid_points)), at)

    specs = [pl.BlockSpec((slab,), lambda i: (0,)), rows_of(height, main_at)]
    args = [index, table]
    if double_last:
        shapes[-1] = (2 * extra, 2 * slab)
        specs.append(rows_of(extra, extra_at))
        args.append(table)
    return pl.pallas_call(
        functools.partial(pick_kernel, sizes),
        grid=(1,),
        in_specs=specs,
        out_specs=[pl.BlockSpec(s, lambda i: (0, 0)) for s in shapes],
        out_shape=[jax.ShapeDtypeStruct(s, jnp.bfloat16) for s in shapes],
        compiler_params=PARAMS,
    )(*args)


class Stream:
    def __init__(self, copies):
        self.copies = [pltpu.make_async_copy(*copy) for copy in copies]
        self.copies[0].start()
        self.taken = 0

    def take(self):
        self.copies[self.taken].wait()
        self.taken += 1
        if self.taken < len(self.copies):
            self.copies[self.taken].start()


def gather_kernel(index_ref, table_ref, w_ref, norm_ref, onehot_ref, buffer, sems):
    slab = index_ref.shape[0]
    freqs = norm_ref.shape[0]
    place = Place(freqs)

    def work(steps, at, with_norm):
        stream = Stream([(table_ref.at[at(i)], buffer.at[i], sems.at[i]) for i in range(steps)])
        onehot_ref[...] = onehot_of(index_ref, table_ref.shape[3])
        for i in range(steps):
            stream.take()
            total = jnp.zeros((1, slab), jnp.float32)
            for part in range(2):
                piece = dot(buffer[i, part], onehot_ref[...])
                w_ref[at(i), :, part * slab : (part + 1) * slab] = piece.astype(jnp.bfloat16)
                if with_norm:
                    total += row_sum(piece * piece)
            if with_norm:
                norm_ref[i : i + 1, :] = total

    @pl.when(place.diag)
    def _():
        work(freqs, lambda i: i, True)

    @pl.when(jnp.logical_not(place.diag))
    def _():
        norm_ref[...] = jnp.zeros_like(norm_ref)
        work(freqs // 2, lambda i: place.first + i, False)


def gather(index, table):
    freqs, _, block, grid_points = table.shape
    slab = index.shape[0]
    return pl.pallas_call(
        gather_kernel,
        in_specs=[VMEM, HBM],
        out_specs=[VMEM, VMEM],
        out_shape=[
            jax.ShapeDtypeStruct((freqs, block, 2 * slab), jnp.bfloat16),
            jax.ShapeDtypeStruct((freqs, slab), jnp.float32),
        ],
        scratch_shapes=[
            pltpu.VMEM((grid_points, slab), jnp.bfloat16),
            pltpu.VMEM((freqs, 2, block, grid_points), jnp.bfloat16),
            pltpu.SemaphoreType.DMA((freqs,)),
        ],
        name="gather",
        compiler_params=PARAMS,
    )(resident(index), table)


def turned(w, w2_ref, start=0):
    slab = w2_ref.shape[1] // 2
    w2_ref[start:, :slab] = -w[start:, slab:]
    w2_ref[start:, slab:] = w[start:, :slab]


def block_stream(items, first, side, cov_ref, buffer, sems, triangle):
    block = buffer.shape[2]
    tile = block // 2
    copies = []
    for i in items:
        for t in range(2):
            rows = pl.ds(pl.multiple_of(side * block + t * tile, tile), tile)
            columns = pl.ds(tile, tile) if triangle and t else pl.ds(0, block)
            target = buffer.at[i, :, pl.ds(t * tile, tile), columns]
            copies.append((cov_ref.at[first + i, :, rows, columns], target, sems.at[2 * i + t]))
    return Stream(copies)


def images_of(items, first, side, cov_ref, w_ref, image_ref, buffer, w2_ref, sems):
    stream = block_stream(items, first, side, cov_ref, buffer, sems, False)
    tile = buffer.shape[2] // 2
    for place, i in enumerate(items):
        w = w_ref.at[first + i]
        turned(w, w2_ref)
        for t in range(2):
            stream.take()
            rows = slice(t * tile, (t + 1) * tile)
            image_ref[place, rows] = dot(buffer[i, 0, rows], w[...]) + dot(buffer[i, 1, rows], w2_ref[...])


def send_kernel(cov_ref, w_ref, image_ref, buffer, w2_ref, sems):
    place = Place(w_ref.shape[0])
    images_of(range(image_ref.shape[0]), place.first, 1 - place.core, cov_ref, w_ref, image_ref, buffer, w2_ref, sems)


def block_scratch(half, block, wide):
    return [
        pltpu.VMEM((half, 2, block, block), jnp.bfloat16),
        pltpu.VMEM((block, wide), jnp.bfloat16),
        pltpu.SemaphoreType.DMA((2 * half,)),
    ]


def send_images(covariance, w):
    freqs, block, wide = w.shape
    half = freqs // 2
    return pl.pallas_call(
        send_kernel,
        in_specs=[HBM, VMEM],
        out_specs=VMEM,
        scratch_shapes=block_scratch(half, block, wide),
        out_shape=jax.ShapeDtypeStruct((half, block, wide), jnp.float32),
        name="send_images",
        compiler_params=PARAMS,
    )(covariance, w)


def own_form(cov, w, w2_ref, stream):
    block, wide = w2_ref.shape
    slab = wide // 2
    tile = block // 2
    turned(w, w2_ref, tile)
    total = jnp.zeros((1, wide), jnp.float32)
    for t in range(2):
        stream.take()
        rows = slice(t * tile, (t + 1) * tile)
        left = w[rows].astype(jnp.float32)
        image = dot(cov[0, rows, rows], w[rows])
        cross = dot(cov[1, rows, rows], w[rows, :slab])
        if t == 0:
            rest = slice(tile, block)
            upper = dot(cov[0, rows, rest], w[rest])
            upper += dot(cov[1, rows, rest], w2_ref[rest])
            image += 2.0 * upper
        total += row_sum(left * image)
        twice = 2.0 * row_sum(left[:, slab:] * cross)
        total += jnp.concatenate([twice, jnp.zeros_like(twice)], axis=1)
    return total


def own_forms(half, first, side, cov_ref, w_ref, quad_ref, buffer, w2_ref, sems, more=None):
    stream = block_stream(range(half), first, side, cov_ref, buffer, sems, True)
    for i in range(half):
        form = own_form(buffer.at[i], w_ref.at[first + i], w2_ref, stream)
        if more is not None:
            form += more(i)
        quad_ref[pl.ds(first + i, 1), :] = form


def keep_kernel(cov_ref, w_ref, image_ref, quad_ref, buffer, w2_ref, sems):
    place = Place(w_ref.shape[0])
    half = quad_ref.shape[0] // 2
    quad_ref[...] = jnp.zeros_like(quad_ref)

    @pl.when(place.diag)
    def _():
        own_forms(half, place.first, place.core, cov_ref, w_ref, quad_ref, buffer, w2_ref, sems)

    @pl.when(jnp.logical_not(place.diag))
    def _():
        images_of([0], place.first, place.core, cov_ref, w_ref, image_ref, buffer, w2_ref, sems)


def keep_images(covariance, w):
    freqs, block, wide = w.shape
    half = freqs // 2
    return pl.pallas_call(
        keep_kernel,
        in_specs=[HBM, VMEM],
        out_specs=[VMEM, VMEM],
        scratch_shapes=block_scratch(half, block, wide),
        out_shape=[
            jax.ShapeDtypeStruct((1, block, wide), jnp.float32),
            jax.ShapeDtypeStruct((freqs, wide), jnp.float32),
        ],
        name="keep_images",
        compiler_params=PARAMS,
    )(covariance, w)


def early_kernel(pieces, spare, n_left, quad_in_ref, cov_ref, w_ref, keep_ref, received_ref, *refs):
    lefts = refs[:n_left]
    out_ref, rest_ref, buffer, w2_ref, sems, image_ref = refs[n_left:]
    freqs, half, block = w_ref.shape[0], received_ref.shape[0], w_ref.shape[1]
    wide = out_ref.shape[1]
    place = Place(freqs)
    out_ref[...] = quad_in_ref[...]

    @pl.when(place.diag)
    def _():
        first = place.other

        def more(i):
            def pair(at, count):
                return w_ref[first + i, pl.ds(at, count)].astype(jnp.float32) * received_ref[i, pl.ds(at, count)]

            return 2.0 * folded(block, wide, pair)

        own_forms(half, first, place.core, cov_ref, w_ref, out_ref, buffer, w2_ref, sems, more)

    @pl.when(jnp.logical_not(place.diag))
    def _():
        to = 0
        images_of([1], place.first, place.core, cov_ref, w_ref, image_ref, buffer, w2_ref, sems)
        for i in range(half):
            own = (keep_ref, image_ref)[i]
            value = jnp.zeros((1, wide), jnp.float32)
            for source, rows, item, row in pieces:
                if item == i:

                    def far(at, count, source=source, row=row, i=i, own=own):
                        side = pl.ds(row + at, count)
                        return lefts[source][pl.ds(at, count)].astype(jnp.float32) * (
                            own[0, side] + received_ref[i, side]
                        )

                    value += folded(rows, wide, far)
            for item, row, rows in spare:
                if item == i:
                    side = slice(row, row + rows)
                    rest_ref[to : to + rows] = own[0, side] + received_ref[i, side]
                    to += rows
            out_ref[pl.ds(place.first + i, 1), :] += 2.0 * value


def early_dots(quad, covariance, w, keep, received, lefts, pieces, spare):
    _, block, wide = w.shape
    half = received.shape[0]
    left_over = sum(rows for _, _, rows in spare)
    return pl.pallas_call(
        functools.partial(early_kernel, pieces, spare, len(lefts)),
        in_specs=[VMEM, HBM] + [VMEM] * (3 + len(lefts)),
        out_specs=[VMEM, VMEM],
        scratch_shapes=[*block_scratch(half, block, wide), pltpu.VMEM((1, block, wide), jnp.float32)],
        out_shape=[
            jax.ShapeDtypeStruct(quad.shape, jnp.float32),
            jax.ShapeDtypeStruct((left_over, wide), jnp.float32),
        ],
        name="early_dots",
        compiler_params=PARAMS,
    )(quad, covariance, w, *map(resident, (keep, received, *lefts)))


def late_kernel(pieces, planes, own, quad_in_ref, norm_ref, rest_ref, *refs):
    lefts, (out_ref, quad_ref) = refs[:-2], refs[-2:]
    freqs, slab = norm_ref.shape
    place = Place(freqs)
    quad_ref[...] = quad_in_ref[...]

    @pl.when(jnp.logical_not(place.diag))
    def _():
        for source, at, rows, item, row in pieces:


            def far(k, count, source=source, at=at, row=row):
                return lefts[source][pl.ds(at + k, count)].astype(jnp.float32) * rest_ref[pl.ds(row + k, count)]

            quad_ref[pl.ds(place.first + item, 1), :] += 2.0 * folded(rows, quad_ref.shape[1], far)

    both = jnp.concatenate([quad_ref[:, :slab] + quad_ref[:, slab:], norm_ref[...]], axis=0)
    for owner in range(slab // own):
        parcel = both[:, owner * own : (owner + 1) * own]
        for z in range(planes):
            at = (owner * planes + z) * 2 * freqs
            out_ref[at : at + 2 * freqs, :own] = parcel


def late_dots(quad, norm, rest, lefts, pieces, owners, planes):
    freqs, slab = norm.shape
    wide = quad.shape[1]
    own = slab // owners
    return pl.pallas_call(
        functools.partial(late_kernel, pieces, planes, own),
        in_specs=[VMEM] * (3 + len(lefts)),
        out_specs=VMEM,
        scratch_shapes=[pltpu.VMEM((freqs, wide), jnp.float32)],
        out_shape=jax.ShapeDtypeStruct((owners * planes * 2 * freqs, -(-own // 128) * 128), jnp.float32),
        name="late_dots",
        compiler_params=PARAMS,
    )(quad, norm, *map(resident, (rest, *lefts)))


def finish_kernel(planes, arrived_ref, power_ref, surface_ref):
    freqs, own = power_ref.shape
    mine = lax.axis_index("freq")
    sources = arrived_ref.shape[0] // (planes * 2 * freqs)
    surface = jnp.zeros_like(surface_ref)
    for z in range(planes):
        total = jnp.zeros((2 * freqs, own), jnp.float32)
        for source in range(sources):
            at = (source * planes + z) * 2 * freqs
            total += arrived_ref[at : at + 2 * freqs, :own]
        power = total[:freqs] / total[freqs:]
        surface += row_sum(power)

        @pl.when(mine == z)
        def _():
            power_ref[...] = power

    surface_ref[...] = surface / (freqs * planes)


def finish(arrived, freqs, planes, own):
    return pl.pallas_call(
        functools.partial(finish_kernel, planes),
        in_specs=[VMEM],
        out_specs=[VMEM, VMEM],
        out_shape=[
            jax.ShapeDtypeStruct((freqs, own), jnp.float32),
            jax.ShapeDtypeStruct((1, own), jnp.float32),
        ],
        name="finish",
        compiler_params=PARAMS,
    )(resident(arrived))


def local(mesh, covariance, replica_table, slab_index):
    rows, cols, planes = (mesh.shape[a] for a in ("row", "col", "freq"))
    freqs, _, row_block, block = covariance.shape
    slab = slab_index.shape[0]
    chips = cols // 2
    if row_block != 2 * block or chips != rows or freqs != 4:
        raise ValueError("unsupported mesh")
    axes = ("row", "col")

    def device(r, q, j):
        return r * cols + 2 * q + j

    def move(x, pairs):
        return lax.ppermute(x, axes, pairs)

    def total(xs):
        return functools.reduce(jnp.add, xs)

    everyone = [(r, q, j) for r in range(rows) for q in range(chips) for j in range(2)]
    core_swap = [(device(r, q, j), device(r, q, 1 - j)) for r, q, j in everyone]

    n = RELAYED
    chunk = [block * c // 16 for c in CHUNKS]
    starts = [sum(chunk[:k]) for k in range(n + 1)]
    tail = block - starts[n]
    shifts = range(1, rows)
    pairs = {}
    for d in shifts:
        out, back, relay = [], [], []
        for r in range(rows):
            for j in range(2):
                other = (r + d) % rows
                out.append((device(r, r, j), device(r, other, j)))
                back.append((device(r, other, j), device(r, r, j)))
                relay.append((device(r, r, j), device(other, r, j)))
        pairs[d] = out, out + back, relay

    slab_index = apart(slab_index)
    replica_table = apart(replica_table)
    hops = {}
    for d in shifts:
        chunks = pick(slab_index, replica_table, d, rows, 0, chunk[:1], False)
        hops[d] = [move(chunks[0], pairs[d][1])]
    for d in shifts:
        sizes = [*chunk[1:], tail]
        chunks = pick(slab_index, replica_table, d, rows, chunk[0], sizes, True)
        hops[d] += [move(chunks[k - 1], pairs[d][1 if k < n else 0]) for k in range(1, n + 1)]

    w, norm = gather(slab_index, replica_table)
    w = resident(w)
    sent = send_images(covariance, w)
    received = move(sent, core_swap)
    relayed = [total([move(hops[d][k], pairs[d][2]) for d in shifts]) for k in range(n)]
    direct = [total([hops[d][k] for d in shifts]) for k in range(n + 1)]
    keep, quad = keep_images(covariance, w)
    early = [(k, chunk[k], 0, starts[k]) for k in range(n)]
    early += [(n + k, chunk[k], 1, starts[k]) for k in range(n - 1)]
    spare = [(0, starts[n], tail), (1, starts[n - 1], chunk[-1] + tail)]
    late = [(0, 0, tail, 0, 0), (0, tail, tail, 1, tail + chunk[-1]), (1, 0, chunk[-1], 1, tail)]
    quad, rest = early_dots(
        quad, covariance, w, keep, received, direct[:n] + relayed[: n - 1], early, spare
    )
    owners = rows * cols
    parcels = late_dots(quad, norm, rest, [direct[n], relayed[-1]], late, owners, planes)
    arrived = lax.all_to_all(parcels, ("row", "col", "freq"), 0, 0, tiled=True)
    power, surface = finish(arrived, freqs, planes, slab // owners)
    return power, surface[0]


def solution(mesh):
    in_specs = (P("freq", None, "row", "col"), P("freq", None, "col", None), P())
    out_specs = (P("freq", ("row", "col")), P(("row", "col")))

    def body(covariance, replica_table, slab_index):
        return local(mesh, covariance, replica_table, slab_index)

    return jax.shard_map(body, mesh=mesh, in_specs=in_specs, out_specs=out_specs, check_vma=False)
```

time: 101 us -> 88.9 us (0.88)
  Pallas kernels: 51.2 us -> 40.8 us
  starting transfers between devices: 15 us -> 19.3 us
  local copies, waits for them, and re-layouts: 4.19 us -> 0.68 us
  waiting for transfers between devices: 16.6 us -> 14.6 us
    pallas_call x6, Pallas kernels: 45.1 us -> 36.6 us  [the longest x1 11 us: send_images(): pl.pallas_call(send_kernel, in_specs=[HBM, VMEM], out_specs=VMEM, scratch...]
    ppermute x6 -> x8, starting transfers between devices: 15 us -> 19.3 us  [move(): return lax.ppermute(x, axes, pairs)]
    unnamed x12 -> x2, local copies, waits for them, and re-layouts: 3.68 us -> 0.68 us
    ppermute x6 -> x8, waiting for transfers between devices: 16.6 us -> 14.6 us  [move(): return lax.ppermute(x, axes, pairs)]
    pallas_call x2, Pallas kernels: 6.02 us -> 4.22 us  [pick(): pl.pallas_call(functools.partial(pick_kernel, sizes), grid=(1,), in_specs...]
  transfers between devices with their start and end apart: 6 -> 8, of which waited for: 2 -> 3; matrix products, arithmetic and copies ran while one was open for 0% -> 0% of each run, Pallas kernels for 27% -> 24%
where the time goes in v2:
time: 88.9 us; the launch traced here: 88.3 us
  Pallas kernels  40.8 us (46%)
  starting transfers between devices  19.3 us (22%)
  waiting for transfers between devices  14.6 us (16%)
  blocking collectives  12.2 us (14%)
    ppermute x8, starting transfers between devices, move(): return lax.ppermute(x, axes, pairs)  19.3 us
    ppermute x8, waiting for transfers between devices, move(): return lax.ppermute(x, axes, pairs)  14.6 us
    all_to_all x1, blocking collectives, local(): arrived = lax.all_to_all(parcels, ('row', 'col', 'freq'), 0, 0, tiled=True)  12.2 us
    pallas_call x1, Pallas kernels, send_images(): pl.pallas_call(send_kernel, in_specs=[HBM, VMEM], out_specs=VMEM, scratch...  11 us
    pallas_call x1, Pallas kernels, early_dots(): pl.pallas_call(functools.partial(early_kernel, pieces, spare, len(lefts))...  8.65 us
    pallas_call x1, Pallas kernels, keep_images(): pl.pallas_call(keep_kernel, in_specs=[HBM, VMEM], out_specs=[VMEM, VMEM],...  8.29 us
    pallas_call x1, Pallas kernels, gather(): pl.pallas_call(gather_kernel, in_specs=[VMEM, HBM], out_specs=[VMEM, VMEM...  7.84 us
    pallas_call x2, Pallas kernels, pick(): pl.pallas_call(functools.partial(pick_kernel, sizes), grid=(1,), in_specs...  4.22 us
  transfers between devices with their start and end apart: 8, of which 3 were waited for; matrix products, arithmetic and copies ran while one was open for 0% of the time, Pallas kernels for 24%

profile of v2, /device:TPU:0, one launch (start us, length us, event | category | flops | bytes accessed | tf_op | source)
XLA Modules:
  0.0 88.3 jit_solution(15872914370745324122)
XLA Ops:
  0.6 0.0 copy-start
  0.6 0.7 copy-done
  1.3 7.8 %gather.1 = (bf16[4,1024,768]{2,1,0:T(8,128)(2,1)S(1)}, f32[4,384]{1,0:T(4,128)S(1)}) custom-call(s32[384]{0:T(512)S(1)} %copy-done, bf16[4,2,1024,512]{3,2,1,0:T(8,128)(2,1)} %refs_0_.1), custom_call_target="tpu_custom_call" | custom-call | tf_op jit(solution)/shard_map/gather/pallas_call | solution.py:168
  9.2 11.0 %send_images.1 = f32[2,1024,768]{2,1,0:T(8,128)S(1)} custom-call(bf16[4,2,2048,1024]{3,2,1,0:T(8,128)(2,1)} %cov_ref.5, bf16[4,1024,768]{2,1,0:T(8,128)(2,1)S(1)} %get-tuple-element.13.w_ref), custom_call_target="tpu_custom_call" | custom-call | tf_op jit(solution)/shard_map/send_images/pallas_call | solution.py:233
  20.2 0.6 collective-permute-start
  20.7 2.7 %shard_map.51 = (bf16[320,768]{1,0:T(8,128)(2,1)S(1)}, bf16[256,768]{1,0:T(8,128)(2,1)S(1)}, bf16[384,768]{1,0:T(8,128)(2,1)S(1)}) custom-call(s32[384]{0:T(512)} %index_ref.5, bf16[4,2,1024,512]{3,2,1,0:T(8,128)(2,1)} %refs_0_.1, bf16[4,2,1024,512]{3,2,1,0:T(8,128)(2,1)} %refs_0_.1), custom_call_target="tpu_custom_call" | custom-call | tf_op jit(solution)/shard_map/pallas_call | solution.py:113
  23.4 0.1 collective-permute-start.2
  23.5 1.5 %shard_map.50 = bf16[256,768]{1,0:T(8,128)(2,1)S(1)} custom-call(s32[384]{0:T(512)} %index_ref.5, bf16[4,2,1024,512]{3,2,1,0:T(8,128)(2,1)} %refs_0_.1), custom_call_target="tpu_custom_call" | custom-call | tf_op jit(solution)/shard_map/pallas_call | solution.py:113
  25.0 2.1 %collective-permute-start.1 = (bf16[256,768]{1,0:T(8,128)(2,1)S(1)}, bf16[256,768]{1,0:T(8,128)(2,1)S(1)}, u32[]{:S(2)}, u32[]{:S(2)}) collective-permute-start(bf16[256,768]{1,0:T(8,128)(2,1)S(1)} %shard_map.50), channel_id=1, source_target_pairs={{0,8},{4,12},{24,16},{28,20},{8,0},{12,4},{16,24},{20,28},{1,9},{5... | collective-permute-start | bytes 1179656 | tf_op jit(solution)/shard_map/ppermute | solution.py:456
  27.1 0.1 collective-permute-start.3
  27.2 3.9 %collective-permute-start.6 = (bf16[384,768]{1,0:T(8,128)(2,1)S(1)}, bf16[384,768]{1,0:T(8,128)(2,1)S(1)}, u32[]{:S(2)}, u32[]{:S(2)}) collective-permute-start(bf16[384,768]{1,0:T(8,128)(2,1)S(1)} %get-tuple-element.21), channel_id=1, source_target_pairs={{0,8},{4,12},{24,16},{28,20},{1,9},{5,13},{25,17},{29,21},{2,10},{... | collective-permute-start | bytes 1769480 | tf_op jit(solution)/shard_map/ppermute | solution.py:456
  31.1 6.5 %collective-permute-done.2.refs_1_ = bf16[320,768]{1,0:T(8,128)(2,1)S(1)} collective-permute-done((bf16[320,768]{1,0:T(8,128)(2,1)S(1)}, bf16[320,768]{1,0:T(8,128)(2,1)S(1)}, u32[]{:S(2)}, u32[]{:S(2)}) %collective-permute-start.2) | collective-permute-done | bytes 491552 | tf_op jit(solution)/shard_map/ppermute | solution.py:456
  37.6 3.9 %collective-permute-start.5 = (bf16[320,768]{1,0:T(8,128)(2,1)S(1)}, bf16[320,768]{1,0:T(8,128)(2,1)S(1)}, u32[]{:S(2)}, u32[]{:S(2)}) collective-permute-start(bf16[320,768]{1,0:T(8,128)(2,1)S(1)} %collective-permute-done.2.refs_1_), channel_id=1, source_target_pairs={{0,16},{4,20},{24,8},{28,12},{1,17},{5,21},{25,9},{29,13},{2,18},{... | collective-permute-start | bytes 1474568 | tf_op jit(solution)/shard_map/ppermute | solution.py:456
  41.5 4.5 %collective-permute-done.1.refs_0_ = bf16[256,768]{1,0:T(8,128)(2,1)S(1)} collective-permute-done((bf16[256,768]{1,0:T(8,128)(2,1)S(1)}, bf16[256,768]{1,0:T(8,128)(2,1)S(1)}, u32[]{:S(2)}, u32[]{:S(2)}) %collective-permute-start.1) | collective-permute-done | bytes 393248 | tf_op jit(solution)/shard_map/ppermute | solution.py:456
  46.0 3.9 %collective-permute-start.4 = (bf16[256,768]{1,0:T(8,128)(2,1)S(1)}, bf16[256,768]{1,0:T(8,128)(2,1)S(1)}, u32[]{:S(2)}, u32[]{:S(2)}) collective-permute-start(bf16[256,768]{1,0:T(8,128)(2,1)S(1)} %collective-permute-done.1.refs_0_), channel_id=1, source_target_pairs={{0,16},{4,20},{24,8},{28,12},{1,17},{5,21},{25,9},{29,13},{2,18},{... | collective-permute-start | bytes 1179656 | tf_op jit(solution)/shard_map/ppermute | solution.py:456
  49.9 3.6 %collective-permute-done.3.refs_2_ = bf16[256,768]{1,0:T(8,128)(2,1)S(1)} collective-permute-done((bf16[256,768]{1,0:T(8,128)(2,1)S(1)}, bf16[256,768]{1,0:T(8,128)(2,1)S(1)}, u32[]{:S(2)}, u32[]{:S(2)}) %collective-permute-start.3) | collective-permute-done | bytes 393248 | tf_op jit(solution)/shard_map/ppermute | solution.py:456
  53.5 4.9 %collective-permute-start.7 = (bf16[256,768]{1,0:T(8,128)(2,1)S(1)}, bf16[256,768]{1,0:T(8,128)(2,1)S(1)}, u32[]{:S(2)}, u32[]{:S(2)}) collective-permute-start(bf16[256,768]{1,0:T(8,128)(2,1)S(1)} %collective-permute-done.3.refs_2_), channel_id=1, source_target_pairs={{0,16},{4,20},{24,8},{28,12},{1,17},{5,21},{25,9},{29,13},{2,18},{... | collective-permute-start | bytes 1179656 | tf_op jit(solution)/shard_map/ppermute | solution.py:456
  58.4 8.3 %keep_images.1 = (f32[1,1024,768]{2,1,0:T(8,128)S(1)}, f32[4,768]{1,0:T(4,128)S(1)}) custom-call(bf16[4,2,2048,1024]{3,2,1,0:T(8,128)(2,1)} %cov_ref.5, bf16[4,1024,768]{2,1,0:T(8,128)(2,1)S(1)} %get-tuple-element.13.w_ref), custom_call_target="tpu_custom_call" | custom-call | tf_op jit(solution)/shard_map/keep_images/pallas_call | solution.py:293
  66.6 0.0 collective-permute-done.4.refs_3_
  66.7 0.0 collective-permute-done.5.refs_4_
  66.7 0.0 collective-permute-done.received_ref
  66.7 8.6 %early_dots.1 = (f32[4,768]{1,0:T(4,128)S(1)}, f32[640,768]{1,0:T(8,128)S(1)}) custom-call(f32[4,768]{1,0:T(4,128)S(1)} %get-tuple-element.14.quad_in_ref, bf16[4,2,2048,1024]{3,2,1,0:T(8,128)(2,1)} %cov_ref.5, bf16[4,1024,768]{2,1,0:T(8,128)(2,1)S(1)} %get-tuple-element.13.w_ref, f32[1,1024,768]{2,1,0:T(8,128)S(1)} %get-tuple-element.15.keep_ref, ...), custom_call_target="tpu_custom_call" | custom-call | tf_op jit(solution)/shard_map/early_dots/pallas_call | solution.py:356
  75.3 0.0 collective-permute-done.6.refs_0_
  75.3 0.0 collective-permute-done.7.refs_1_
  75.4 0.1 late_dots.1
  75.5 12.2 %all_to_all.11 = f32[32,8,128]{2,1,0:T(8,128)S(1)} all-to-all(f32[32,8,128]{2,1,0:T(8,128)S(1)} %bitcast.4), channel_id=1, replica_groups=mesh['row'=2,'col'=4,'freq'=4] {'row','col','freq'}, dimensions={0} | all-to-all | bytes 262144 | tf_op jit(solution)/shard_map/all_to_all | solution.py:507
  87.6 0.7 finish.1
Async XLA Ops:
  0.6 0.7 copy-start
  20.2 46.5 %collective-permute-start = (f32[2,1024,768]{2,1,0:T(8,128)S(1)}, f32[2,1024,768]{2,1,0:T(8,128)S(1)}, u32[]{:S(2)}, u32[]{:S(2)}) collective-permute-start(f32[2,1024,768]{2,1,0:T(8,128)S(1)} %send_images.1), channel_id=1, source_target_pairs={{0,4},{4,0},{8,12},{12,8},{16,20},{20,16},{24,28},{28,24},{1,5},{5... | collective-permute-start | bytes 18874376 | tf_op jit(solution)/shard_map/ppermute | solution.py:456
  23.4 14.2 %collective-permute-start.2 = (bf16[320,768]{1,0:T(8,128)(2,1)S(1)}, bf16[320,768]{1,0:T(8,128)(2,1)S(1)}, u32[]{:S(2)}, u32[]{:S(2)}) collective-permute-start(bf16[320,768]{1,0:T(8,128)(2,1)S(1)} %get-tuple-element.16), channel_id=1, source_target_pairs={{0,8},{4,12},{24,16},{28,20},{8,0},{12,4},{16,24},{20,28},{1,9},{5... | collective-permute-start | bytes 1474568 | tf_op jit(solution)/shard_map/ppermute | solution.py:456
  25.0 21.0 %collective-permute-start.1 = (bf16[256,768]{1,0:T(8,128)(2,1)S(1)}, bf16[256,768]{1,0:T(8,128)(2,1)S(1)}, u32[]{:S(2)}, u32[]{:S(2)}) collective-permute-start(bf16[256,768]{1,0:T(8,128)(2,1)S(1)} %shard_map.50), channel_id=1, source_target_pairs={{0,8},{4,12},{24,16},{28,20},{8,0},{12,4},{16,24},{20,28},{1,9},{5... | collective-permute-start | bytes 1179656 | tf_op jit(solution)/shard_map/ppermute | solution.py:456
  27.1 26.4 %collective-permute-start.3 = (bf16[256,768]{1,0:T(8,128)(2,1)S(1)}, bf16[256,768]{1,0:T(8,128)(2,1)S(1)}, u32[]{:S(2)}, u32[]{:S(2)}) collective-permute-start(bf16[256,768]{1,0:T(8,128)(2,1)S(1)} %get-tuple-element.17), channel_id=1, source_target_pairs={{0,8},{4,12},{24,16},{28,20},{8,0},{12,4},{16,24},{20,28},{1,9},{5... | collective-permute-start | bytes 1179656 | tf_op jit(solution)/shard_map/ppermute | solution.py:456
  27.2 48.1 %collective-permute-start.6 = (bf16[384,768]{1,0:T(8,128)(2,1)S(1)}, bf16[384,768]{1,0:T(8,128)(2,1)S(1)}, u32[]{:S(2)}, u32[]{:S(2)}) collective-permute-start(bf16[384,768]{1,0:T(8,128)(2,1)S(1)} %get-tuple-element.21), channel_id=1, source_target_pairs={{0,8},{4,12},{24,16},{28,20},{1,9},{5,13},{25,17},{29,21},{2,10},{... | collective-permute-start | bytes 1769480 | tf_op jit(solution)/shard_map/ppermute | solution.py:456
  37.6 29.1 %collective-permute-start.5 = (bf16[320,768]{1,0:T(8,128)(2,1)S(1)}, bf16[320,768]{1,0:T(8,128)(2,1)S(1)}, u32[]{:S(2)}, u32[]{:S(2)}) collective-permute-start(bf16[320,768]{1,0:T(8,128)(2,1)S(1)} %collective-permute-done.2.refs_1_), channel_id=1, source_target_pairs={{0,16},{4,20},{24,8},{28,12},{1,17},{5,21},{25,9},{29,13},{2,18},{... | collective-permute-start | bytes 1474568 | tf_op jit(solution)/shard_map/ppermute | solution.py:456
  46.0 20.6 %collective-permute-start.4 = (bf16[256,768]{1,0:T(8,128)(2,1)S(1)}, bf16[256,768]{1,0:T(8,128)(2,1)S(1)}, u32[]{:S(2)}, u32[]{:S(2)}) collective-permute-start(bf16[256,768]{1,0:T(8,128)(2,1)S(1)} %collective-permute-done.1.refs_0_), channel_id=1, source_target_pairs={{0,16},{4,20},{24,8},{28,12},{1,17},{5,21},{25,9},{29,13},{2,18},{... | collective-permute-start | bytes 1179656 | tf_op jit(solution)/shard_map/ppermute | solution.py:456
  53.5 21.9 %collective-permute-start.7 = (bf16[256,768]{1,0:T(8,128)(2,1)S(1)}, bf16[256,768]{1,0:T(8,128)(2,1)S(1)}, u32[]{:S(2)}, u32[]{:S(2)}) collective-permute-start(bf16[256,768]{1,0:T(8,128)(2,1)S(1)} %collective-permute-done.3.refs_2_), channel_id=1, source_target_pairs={{0,16},{4,20},{24,8},{28,12},{1,17},{5,21},{25,9},{29,13},{2,18},{... | collective-permute-start | bytes 1179656 | tf_op jit(solution)/shard_map/ppermute | solution.py:456

commit v3 on v2

--- a/solution.py
+++ b/solution.py
@@ -8,7 +8,7 @@
 from jax.sharding import PartitionSpec as P
 
 
-CHUNKS = (4, 5, 4)
+CHUNKS = (8, 9, 8)
 RELAYED = len(CHUNKS)
 
 
@@ -120,17 +120,10 @@
     )(*args)
 
 
-class Stream:
-    def __init__(self, copies):
-        self.copies = [pltpu.make_async_copy(*copy) for copy in copies]
-        self.copies[0].start()
-        self.taken = 0
-
-    def take(self):
-        self.copies[self.taken].wait()
-        self.taken += 1
-        if self.taken < len(self.copies):
-            self.copies[self.taken].start()
+def fetch(source, target, sem):
+    copy = pltpu.make_async_copy(source, target, sem)
+    copy.start()
+    return copy
 
 
 def gather_kernel(index_ref, table_ref, w_ref, norm_ref, onehot_ref, buffer, sems):
@@ -139,10 +132,10 @@
     place = Place(freqs)
 
     def work(steps, at, with_norm):
-        stream = Stream([(table_ref.at[at(i)], buffer.at[i], sems.at[i]) for i in range(steps)])
+        copies = [fetch(table_ref.at[at(i)], buffer.at[i], sems.at[i]) for i in range(steps)]
         onehot_ref[...] = onehot_of(index_ref, table_ref.shape[3])
         for i in range(steps):
-            stream.take()
+            copies[i].wait()
             total = jnp.zeros((1, slab), jnp.float32)
             for part in range(2):
                 piece = dot(buffer[i, part], onehot_ref[...])
@@ -189,27 +182,34 @@
     w2_ref[start:, slab:] = w[start:, :slab]
 
 
-def block_stream(items, first, side, cov_ref, buffer, sems, triangle):
+def block_copies(items, first, side, cov_ref, buffer, sems, triangle):
     block = buffer.shape[2]
     tile = block // 2
+    parts = [(0, tile, 0), (tile, tile, tile)] if triangle else [(0, block, 0)]
     copies = []
     for i in items:
-        for t in range(2):
-            rows = pl.ds(pl.multiple_of(side * block + t * tile, tile), tile)
-            columns = pl.ds(tile, tile) if triangle and t else pl.ds(0, block)
-            target = buffer.at[i, :, pl.ds(t * tile, tile), columns]
-            copies.append((cov_ref.at[first + i, :, rows, columns], target, sems.at[2 * i + t]))
-    return Stream(copies)
+        for t, (row, rows, column) in enumerate(parts):
+            columns = pl.ds(column, block - column)
+            source = cov_ref.at[first + i, :, pl.ds(pl.multiple_of(side * block + row, tile), rows), columns]
+            target = buffer.at[i, :, pl.ds(row, rows), columns]
+            copies.append((i, fetch(source, target, sems.at[2 * i + t])))
+    return copies
+
+
+def arrive(copies, item):
+    for i, copy in copies:
+        if i == item:
+            copy.wait()
 
 
 def images_of(items, first, side, cov_ref, w_ref, image_ref, buffer, w2_ref, sems):
-    stream = block_stream(items, first, side, cov_ref, buffer, sems, False)
+    copies = block_copies(items, first, side, cov_ref, buffer, sems, False)
     tile = buffer.shape[2] // 2
     for place, i in enumerate(items):
         w = w_ref.at[first + i]
         turned(w, w2_ref)
+        arrive(copies, i)
         for t in range(2):
-            stream.take()
             rows = slice(t * tile, (t + 1) * tile)
             image_ref[place, rows] = dot(buffer[i, 0, rows], w[...]) + dot(buffer[i, 1, rows], w2_ref[...])
 
@@ -241,14 +241,13 @@
     )(covariance, w)
 
 
-def own_form(cov, w, w2_ref, stream):
+def own_form(cov, w, w2_ref):
     block, wide = w2_ref.shape
     slab = wide // 2
     tile = block // 2
     turned(w, w2_ref, tile)
     total = jnp.zeros((1, wide), jnp.float32)
     for t in range(2):
-        stream.take()
         rows = slice(t * tile, (t + 1) * tile)
         left = w[rows].astype(jnp.float32)
         image = dot(cov[0, rows, rows], w[rows])
@@ -265,9 +264,10 @@
 
 
 def own_forms(half, first, side, cov_ref, w_ref, quad_ref, buffer, w2_ref, sems, more=None):
-    stream = block_stream(range(half), first, side, cov_ref, buffer, sems, True)
+    copies = block_copies(range(half), first, side, cov_ref, buffer, sems, True)
     for i in range(half):
-        form = own_form(buffer.at[i], w_ref.at[first + i], w2_ref, stream)
+        arrive(copies, i)
+        form = own_form(buffer.at[i], w_ref.at[first + i], w2_ref)
         if more is not None:
             form += more(i)
         quad_ref[pl.ds(first + i, 1), :] = form
@@ -383,12 +383,12 @@
 
             quad_ref[pl.ds(place.first + item, 1), :] += 2.0 * folded(rows, quad_ref.shape[1], far)
 
-    both = jnp.concatenate([quad_ref[:, :slab] + quad_ref[:, slab:], norm_ref[...]], axis=0)
+    quad, norm = quad_ref[:, :slab] + quad_ref[:, slab:], norm_ref[...]
     for owner in range(slab // own):
-        parcel = both[:, owner * own : (owner + 1) * own]
+        mine = slice(owner * own, (owner + 1) * own)
+        parcel = jnp.concatenate([quad[:, mine], norm[:, mine]], axis=1)
         for z in range(planes):
-            at = (owner * planes + z) * 2 * freqs
-            out_ref[at : at + 2 * freqs, :own] = parcel
+            out_ref[owner * planes + z, :, : 2 * own] = parcel
 
 
 def late_dots(quad, norm, rest, lefts, pieces, owners, planes):
@@ -400,7 +400,7 @@
         in_specs=[VMEM] * (3 + len(lefts)),
         out_specs=VMEM,
         scratch_shapes=[pltpu.VMEM((freqs, wide), jnp.float32)],
-        out_shape=jax.ShapeDtypeStruct((owners * planes * 2 * freqs, -(-own // 128) * 128), jnp.float32),
+        out_shape=jax.ShapeDtypeStruct((owners * planes, freqs, -(-2 * own // 128) * 128), jnp.float32),
         name="late_dots",
         compiler_params=PARAMS,
     )(quad, norm, *map(resident, (rest, *lefts)))
@@ -409,14 +409,12 @@
 def finish_kernel(planes, arrived_ref, power_ref, surface_ref):
     freqs, own = power_ref.shape
     mine = lax.axis_index("freq")
-    sources = arrived_ref.shape[0] // (planes * 2 * freqs)
     surface = jnp.zeros_like(surface_ref)
     for z in range(planes):
-        total = jnp.zeros((2 * freqs, own), jnp.float32)
-        for source in range(sources):
-            at = (source * planes + z) * 2 * freqs
-            total += arrived_ref[at : at + 2 * freqs, :own]
-        power = total[:freqs] / total[freqs:]
+        total = arrived_ref[z]
+        for source in range(planes + z, arrived_ref.shape[0], planes):
+            total += arrived_ref[source]
+        power = total[:, :own] / total[:, own : 2 * own]
         surface += row_sum(power)
 
         @pl.when(mine == z)
@@ -462,7 +460,7 @@
     core_swap = [(device(r, q, j), device(r, q, 1 - j)) for r, q, j in everyone]
 
     n = RELAYED
-    chunk = [block * c // 16 for c in CHUNKS]
+    chunk = [block * c // 32 // 16 * 16 for c in CHUNKS]
     starts = [sum(chunk[:k]) for k in range(n + 1)]
     tail = block - starts[n]
     shifts = range(1, rows)
@@ -495,15 +493,17 @@
     relayed = [total([move(hops[d][k], pairs[d][2]) for d in shifts]) for k in range(n)]
     direct = [total([hops[d][k] for d in shifts]) for k in range(n + 1)]
     keep, quad = keep_images(covariance, w)
+    hold = n - 2
     early = [(k, chunk[k], 0, starts[k]) for k in range(n)]
-    early += [(n + k, chunk[k], 1, starts[k]) for k in range(n - 1)]
-    spare = [(0, starts[n], tail), (1, starts[n - 1], chunk[-1] + tail)]
-    late = [(0, 0, tail, 0, 0), (0, tail, tail, 1, tail + chunk[-1]), (1, 0, chunk[-1], 1, tail)]
+    early += [(n + k, chunk[k], 1, starts[k]) for k in range(hold)]
+    spare = [(0, starts[n], tail), (1, starts[hold], block - starts[hold])]
+    late = [(0, 0, tail, 0, 0), (0, tail, tail, 1, tail + starts[n] - starts[hold])]
+    late += [(1 + k - hold, 0, chunk[k], 1, tail + starts[k] - starts[hold]) for k in range(hold, n)]
     quad, rest = early_dots(
-        quad, covariance, w, keep, received, direct[:n] + relayed[: n - 1], early, spare
+        quad, covariance, w, keep, received, direct[:n] + relayed[:hold], early, spare
     )
     owners = rows * cols
-    parcels = late_dots(quad, norm, rest, [direct[n], relayed[-1]], late, owners, planes)
+    parcels = late_dots(quad, norm, rest, [direct[n], *relayed[hold:]], late, owners, planes)
     arrived = lax.all_to_all(parcels, ("row", "col", "freq"), 0, 0, tiled=True)
     power, surface = finish(arrived, freqs, planes, slab // owners)
     return power, surface[0]

time: 88.9 us -> 82.4 us (0.927)
  Pallas kernels: 40.8 us -> 36.5 us
  waiting for transfers between devices: 14.6 us -> 13.5 us
  blocking collectives: 12.2 us -> 11.3 us
    pallas_call x1, Pallas kernels: 11 us -> 9.23 us  [send_images(): pl.pallas_call(send_kernel, in_specs=[HBM, VMEM], out_specs=VMEM, scratch...]
    pallas_call x1, Pallas kernels: 8.29 us -> 7.1 us  [keep_images(): pl.pallas_call(keep_kernel, in_specs=[HBM, VMEM], out_specs=[VMEM, VMEM],...]
    ppermute x8, waiting for transfers between devices: 14.6 us -> 13.5 us  [move(): return lax.ppermute(x, axes, pairs)]
    pallas_call x1, Pallas kernels: 7.84 us -> 6.86 us  [gather(): pl.pallas_call(gather_kernel, in_specs=[VMEM, HBM], out_specs=[VMEM, VMEM...]
where the time goes in v3:
time: 82.4 us; the launch traced here: 82.1 us
  Pallas kernels  36.5 us (44%)
  starting transfers between devices  19.4 us (24%)
  waiting for transfers between devices  13.5 us (16%)
  blocking collectives  11.3 us (14%)
    ppermute x8, starting transfers between devices, move(): return lax.ppermute(x, axes, pairs)  19.4 us
    ppermute x8, waiting for transfers between devices, move(): return lax.ppermute(x, axes, pairs)  13.5 us
    all_to_all x1, blocking collectives, local(): arrived = lax.all_to_all(parcels, ('row', 'col', 'freq'), 0, 0, tiled=True)  11.3 us
    pallas_call x1, Pallas kernels, send_images(): pl.pallas_call(send_kernel, in_specs=[HBM, VMEM], out_specs=VMEM, scratch...  9.23 us
    pallas_call x1, Pallas kernels, early_dots(): pl.pallas_call(functools.partial(early_kernel, pieces, spare, len(lefts))...  7.96 us
    pallas_call x1, Pallas kernels, keep_images(): pl.pallas_call(keep_kernel, in_specs=[HBM, VMEM], out_specs=[VMEM, VMEM],...  7.1 us
    pallas_call x1, Pallas kernels, gather(): pl.pallas_call(gather_kernel, in_specs=[VMEM, HBM], out_specs=[VMEM, VMEM...  6.86 us
    pallas_call x2, Pallas kernels, pick(): pl.pallas_call(functools.partial(pick_kernel, sizes), grid=(1,), in_specs...  4.28 us
  transfers between devices with their start and end apart: 8, of which 3 were waited for; matrix products, arithmetic and copies ran while one was open for 0% of the time, Pallas kernels for 24%

profile of v3, /device:TPU:0, one launch (start us, length us, event | category | flops | bytes accessed | tf_op | source)
XLA Modules:
  0.0 82.1 jit_solution(13769534536511080434)
XLA Ops:
  0.6 0.0 copy-start
  0.6 0.7 copy-done
  1.3 6.9 %gather.1 = (bf16[4,1024,768]{2,1,0:T(8,128)(2,1)S(1)}, f32[4,384]{1,0:T(4,128)S(1)}) custom-call(s32[384]{0:T(512)S(1)} %copy-done, bf16[4,2,1024,512]{3,2,1,0:T(8,128)(2,1)} %refs_0_.1), custom_call_target="tpu_custom_call" | custom-call | tf_op jit(solution)/shard_map/gather/pallas_call | solution.py:161
  8.2 9.2 %send_images.1 = f32[2,1024,768]{2,1,0:T(8,128)S(1)} custom-call(bf16[4,2,2048,1024]{3,2,1,0:T(8,128)(2,1)} %cov_ref.5, bf16[4,1024,768]{2,1,0:T(8,128)(2,1)S(1)} %get-tuple-element.13.w_ref), custom_call_target="tpu_custom_call" | custom-call | tf_op jit(solution)/shard_map/send_images/pallas_call | solution.py:233
  17.4 0.6 collective-permute-start
  18.0 2.7 %shard_map.51 = (bf16[288,768]{1,0:T(8,128)(2,1)S(1)}, bf16[256,768]{1,0:T(8,128)(2,1)S(1)}, bf16[448,768]{1,0:T(8,128)(2,1)S(1)}) custom-call(s32[384]{0:T(512)} %index_ref.5, bf16[4,2,1024,512]{3,2,1,0:T(8,128)(2,1)} %refs_0_.1, bf16[4,2,1024,512]{3,2,1,0:T(8,128)(2,1)} %refs_0_.1), custom_call_target="tpu_custom_call" | custom-call | tf_op jit(solution)/shard_map/pallas_call | solution.py:113
  20.7 0.1 collective-permute-start.2
  20.8 1.5 %shard_map.50 = bf16[256,768]{1,0:T(8,128)(2,1)S(1)} custom-call(s32[384]{0:T(512)} %index_ref.5, bf16[4,2,1024,512]{3,2,1,0:T(8,128)(2,1)} %refs_0_.1), custom_call_target="tpu_custom_call" | custom-call | tf_op jit(solution)/shard_map/pallas_call | solution.py:113
  22.3 2.1 %collective-permute-start.1 = (bf16[256,768]{1,0:T(8,128)(2,1)S(1)}, bf16[256,768]{1,0:T(8,128)(2,1)S(1)}, u32[]{:S(2)}, u32[]{:S(2)}) collective-permute-start(bf16[256,768]{1,0:T(8,128)(2,1)S(1)} %shard_map.50), channel_id=1, source_target_pairs={{0,8},{4,12},{24,16},{28,20},{8,0},{12,4},{16,24},{20,28},{1,9},{5... | collective-permute-start | bytes 1179656 | tf_op jit(solution)/shard_map/ppermute | solution.py:454
  24.4 0.1 collective-permute-start.3
  24.5 3.9 %collective-permute-start.5 = (bf16[448,768]{1,0:T(8,128)(2,1)S(1)}, bf16[448,768]{1,0:T(8,128)(2,1)S(1)}, u32[]{:S(2)}, u32[]{:S(2)}) collective-permute-start(bf16[448,768]{1,0:T(8,128)(2,1)S(1)} %get-tuple-element.21), channel_id=1, source_target_pairs={{0,8},{4,12},{24,16},{28,20},{1,9},{5,13},{25,17},{29,21},{2,10},{... | collective-permute-start | bytes 2064392 | tf_op jit(solution)/shard_map/ppermute | solution.py:454
  28.4 5.4 %collective-permute-done.2.refs_1_ = bf16[288,768]{1,0:T(8,128)(2,1)S(1)} collective-permute-done((bf16[288,768]{1,0:T(8,128)(2,1)S(1)}, bf16[288,768]{1,0:T(8,128)(2,1)S(1)}, u32[]{:S(2)}, u32[]{:S(2)}) %collective-permute-start.2) | collective-permute-done | bytes 442400 | tf_op jit(solution)/shard_map/ppermute | solution.py:454
  33.8 3.9 %collective-permute-start.6 = (bf16[288,768]{1,0:T(8,128)(2,1)S(1)}, bf16[288,768]{1,0:T(8,128)(2,1)S(1)}, u32[]{:S(2)}, u32[]{:S(2)}) collective-permute-start(bf16[288,768]{1,0:T(8,128)(2,1)S(1)} %collective-permute-done.2.refs_1_), channel_id=1, source_target_pairs={{0,16},{4,20},{24,8},{28,12},{1,17},{5,21},{25,9},{29,13},{2,18},{... | collective-permute-start | bytes 1327112 | tf_op jit(solution)/shard_map/ppermute | solution.py:454
  37.8 4.5 %collective-permute-done.1.refs_0_ = bf16[256,768]{1,0:T(8,128)(2,1)S(1)} collective-permute-done((bf16[256,768]{1,0:T(8,128)(2,1)S(1)}, bf16[256,768]{1,0:T(8,128)(2,1)S(1)}, u32[]{:S(2)}, u32[]{:S(2)}) %collective-permute-start.1) | collective-permute-done | bytes 393248 | tf_op jit(solution)/shard_map/ppermute | solution.py:454
  42.3 3.9 %collective-permute-start.4 = (bf16[256,768]{1,0:T(8,128)(2,1)S(1)}, bf16[256,768]{1,0:T(8,128)(2,1)S(1)}, u32[]{:S(2)}, u32[]{:S(2)}) collective-permute-start(bf16[256,768]{1,0:T(8,128)(2,1)S(1)} %collective-permute-done.1.refs_0_), channel_id=1, source_target_pairs={{0,16},{4,20},{24,8},{28,12},{1,17},{5,21},{25,9},{29,13},{2,18},{... | collective-permute-start | bytes 1179656 | tf_op jit(solution)/shard_map/ppermute | solution.py:454
  46.2 3.6 %collective-permute-done.3.refs_2_ = bf16[256,768]{1,0:T(8,128)(2,1)S(1)} collective-permute-done((bf16[256,768]{1,0:T(8,128)(2,1)S(1)}, bf16[256,768]{1,0:T(8,128)(2,1)S(1)}, u32[]{:S(2)}, u32[]{:S(2)}) %collective-permute-start.3) | collective-permute-done | bytes 393248 | tf_op jit(solution)/shard_map/ppermute | solution.py:454
  49.7 4.9 %collective-permute-start.7 = (bf16[256,768]{1,0:T(8,128)(2,1)S(1)}, bf16[256,768]{1,0:T(8,128)(2,1)S(1)}, u32[]{:S(2)}, u32[]{:S(2)}) collective-permute-start(bf16[256,768]{1,0:T(8,128)(2,1)S(1)} %collective-permute-done.3.refs_2_), channel_id=1, source_target_pairs={{0,16},{4,20},{24,8},{28,12},{1,17},{5,21},{25,9},{29,13},{2,18},{... | collective-permute-start | bytes 1179656 | tf_op jit(solution)/shard_map/ppermute | solution.py:454
  54.6 7.1 %keep_images.1 = (f32[1,1024,768]{2,1,0:T(8,128)S(1)}, f32[4,768]{1,0:T(4,128)S(1)}) custom-call(bf16[4,2,2048,1024]{3,2,1,0:T(8,128)(2,1)} %cov_ref.5, bf16[4,1024,768]{2,1,0:T(8,128)(2,1)S(1)} %get-tuple-element.13.w_ref), custom_call_target="tpu_custom_call" | custom-call | tf_op jit(solution)/shard_map/keep_images/pallas_call | solution.py:293
  61.7 0.0 collective-permute-done.4.refs_3_
  61.7 0.0 collective-permute-done.received_ref
  61.7 8.0 %early_dots.1 = (f32[4,768]{1,0:T(4,128)S(1)}, f32[992,768]{1,0:T(8,128)S(1)}) custom-call(f32[4,768]{1,0:T(4,128)S(1)} %get-tuple-element.14.quad_in_ref, bf16[4,2,2048,1024]{3,2,1,0:T(8,128)(2,1)} %cov_ref.5, bf16[4,1024,768]{2,1,0:T(8,128)(2,1)S(1)} %get-tuple-element.13.w_ref, f32[1,1024,768]{2,1,0:T(8,128)S(1)} %get-tuple-element.15.keep_ref, ...), custom_call_target="tpu_custom_call" | custom-call | tf_op jit(solution)/shard_map/early_dots/pallas_call | solution.py:356
  69.7 0.0 collective-permute-done.5.refs_0_
  69.7 0.0 collective-permute-done.7.refs_2_
  69.7 0.0 collective-permute-done.6.refs_1_
  69.7 0.1 late_dots.1
  69.8 11.3 %all_to_all.5.arrived_ref = f32[32,4,128]{2,1,0:T(4,128)S(1)} all-to-all(f32[32,4,128]{2,1,0:T(4,128)S(1)} %late_dots.1), channel_id=1, replica_groups=mesh['row'=2,'col'=4,'freq'=4] {'row','col','freq'}, dimensions={0} | all-to-all | bytes 131072 | tf_op jit(solution)/shard_map/all_to_all | solution.py:507
  81.1 0.9 %finish.1 = (f32[4,48]{1,0:T(4,128)}, f32[1,48]{1,0:T(1,128)}) custom-call(f32[32,4,128]{2,1,0:T(4,128)S(1)} %all_to_all.5.arrived_ref), custom_call_target="tpu_custom_call" | custom-call | tf_op jit(solution)/shard_map/finish/pallas_call | solution.py:428
Async XLA Ops:
  0.6 0.7 copy-start
  17.4 44.3 %collective-permute-start = (f32[2,1024,768]{2,1,0:T(8,128)S(1)}, f32[2,1024,768]{2,1,0:T(8,128)S(1)}, u32[]{:S(2)}, u32[]{:S(2)}) collective-permute-start(f32[2,1024,768]{2,1,0:T(8,128)S(1)} %send_images.1), channel_id=1, source_target_pairs={{0,4},{4,0},{8,12},{12,8},{16,20},{20,16},{24,28},{28,24},{1,5},{5... | collective-permute-start | bytes 18874376 | tf_op jit(solution)/shard_map/ppermute | solution.py:454
  20.7 13.1 %collective-permute-start.2 = (bf16[288,768]{1,0:T(8,128)(2,1)S(1)}, bf16[288,768]{1,0:T(8,128)(2,1)S(1)}, u32[]{:S(2)}, u32[]{:S(2)}) collective-permute-start(bf16[288,768]{1,0:T(8,128)(2,1)S(1)} %get-tuple-element.16), channel_id=1, source_target_pairs={{0,8},{4,12},{24,16},{28,20},{8,0},{12,4},{16,24},{20,28},{1,9},{5... | collective-permute-start | bytes 1327112 | tf_op jit(solution)/shard_map/ppermute | solution.py:454
  22.3 19.9 %collective-permute-start.1 = (bf16[256,768]{1,0:T(8,128)(2,1)S(1)}, bf16[256,768]{1,0:T(8,128)(2,1)S(1)}, u32[]{:S(2)}, u32[]{:S(2)}) collective-permute-start(bf16[256,768]{1,0:T(8,128)(2,1)S(1)} %shard_map.50), channel_id=1, source_target_pairs={{0,8},{4,12},{24,16},{28,20},{8,0},{12,4},{16,24},{20,28},{1,9},{5... | collective-permute-start | bytes 1179656 | tf_op jit(solution)/shard_map/ppermute | solution.py:454
  24.4 25.3 %collective-permute-start.3 = (bf16[256,768]{1,0:T(8,128)(2,1)S(1)}, bf16[256,768]{1,0:T(8,128)(2,1)S(1)}, u32[]{:S(2)}, u32[]{:S(2)}) collective-permute-start(bf16[256,768]{1,0:T(8,128)(2,1)S(1)} %get-tuple-element.17), channel_id=1, source_target_pairs={{0,8},{4,12},{24,16},{28,20},{8,0},{12,4},{16,24},{20,28},{1,9},{5... | collective-permute-start | bytes 1179656 | tf_op jit(solution)/shard_map/ppermute | solution.py:454
  24.5 45.2 %collective-permute-start.5 = (bf16[448,768]{1,0:T(8,128)(2,1)S(1)}, bf16[448,768]{1,0:T(8,128)(2,1)S(1)}, u32[]{:S(2)}, u32[]{:S(2)}) collective-permute-start(bf16[448,768]{1,0:T(8,128)(2,1)S(1)} %get-tuple-element.21), channel_id=1, source_target_pairs={{0,8},{4,12},{24,16},{28,20},{1,9},{5,13},{25,17},{29,21},{2,10},{... | collective-permute-start | bytes 2064392 | tf_op jit(solution)/shard_map/ppermute | solution.py:454
  33.8 35.9 %collective-permute-start.6 = (bf16[288,768]{1,0:T(8,128)(2,1)S(1)}, bf16[288,768]{1,0:T(8,128)(2,1)S(1)}, u32[]{:S(2)}, u32[]{:S(2)}) collective-permute-start(bf16[288,768]{1,0:T(8,128)(2,1)S(1)} %collective-permute-done.2.refs_1_), channel_id=1, source_target_pairs={{0,16},{4,20},{24,8},{28,12},{1,17},{5,21},{25,9},{29,13},{2,18},{... | collective-permute-start | bytes 1327112 | tf_op jit(solution)/shard_map/ppermute | solution.py:454
  42.3 19.5 %collective-permute-start.4 = (bf16[256,768]{1,0:T(8,128)(2,1)S(1)}, bf16[256,768]{1,0:T(8,128)(2,1)S(1)}, u32[]{:S(2)}, u32[]{:S(2)}) collective-permute-start(bf16[256,768]{1,0:T(8,128)(2,1)S(1)} %collective-permute-done.1.refs_0_), channel_id=1, source_target_pairs={{0,16},{4,20},{24,8},{28,12},{1,17},{5,21},{25,9},{29,13},{2,18},{... | collective-permute-start | bytes 1179656 | tf_op jit(solution)/shard_map/ppermute | solution.py:454
  49.7 20.0 %collective-permute-start.7 = (bf16[256,768]{1,0:T(8,128)(2,1)S(1)}, bf16[256,768]{1,0:T(8,128)(2,1)S(1)}, u32[]{:S(2)}, u32[]{:S(2)}) collective-permute-start(bf16[256,768]{1,0:T(8,128)(2,1)S(1)} %collective-permute-done.3.refs_2_), channel_id=1, source_target_pairs={{0,16},{4,20},{24,8},{28,12},{1,17},{5,21},{25,9},{29,13},{2,18},{... | collective-permute-start | bytes 1179656 | tf_op jit(solution)/shard_map/ppermute | solution.py:454
